TPU v7x, 32 devices: a whole 2x2x4 slice. The times are simulated.
32 devices in a mesh: dp: 2 (over y), row: 4 (over z), col: 4 (over x, core).
Axes of the slice: x: 2, y: 2, z: 4, core: 2. Of those that a mesh axis runs over, the one named last changes fastest.
Arguments:
- hidden_in: float32 [2048, 1024], P(('dp', 'col'), 'row'), may hold values from -6 to 6
- segments: int32 [2, 1024], P('dp'), may hold values from 0 to 2, never falling along the last dimension, each value on 1 to 600 neighbouring positions
- norm_in: float32 [1024], P('row'), may hold values from 0.5 to 1.5
- w_query: bfloat16 [1024, 1024], P('row', 'col'), may hold values from -0.1875 to 0.1875
- w_key: bfloat16 [1024, 512], P('row', 'col'), may hold values from -0.1875 to 0.1875
- w_value: bfloat16 [1024, 512], P('row', 'col'), may hold values from -0.1875 to 0.1875
- query_gain: float32 [64], replicated, may hold values from 0.5 to 1.5
- key_gain: float32 [64], replicated, may hold values from 0.5 to 1.5
- w_out: bfloat16 [1024, 1024], P('col', 'row'), may hold values from -0.75 to 0.75
- norm_mid: float32 [1024], P('row'), may hold values from 0.5 to 1.5
- w_gate: bfloat16 [1024, 4608], P('row', 'col'), may hold values from -0.1875 to 0.1875
- w_up: bfloat16 [1024, 4608], P('row', 'col'), may hold values from -0.1875 to 0.1875
- w_down: bfloat16 [4608, 1024], P('col', 'row'), may hold values from -0.15625 to 0.15625
- cotangent: float32 [2048, 1024], P(('dp', 'col'), 'row'), may hold values from -6 to 6
Outputs:
- output: float32 [2048, 1024], P(('dp', 'col'), 'row')
- grad_hidden: float32 [2048, 1024], P(('dp', 'col'), 'row')
- grad_norm_in: float32 [1024], P('row')
- grad_query: float32 [1024, 1024], P('row', 'col')
- grad_key: float32 [1024, 512], P('row', 'col')
- grad_value: float32 [1024, 512], P('row', 'col')
- grad_query_gain: float32 [64], replicated
- grad_key_gain: float32 [64], replicated
- grad_out: float32 [1024, 1024], P('col', 'row')
- grad_norm_mid: float32 [1024], P('row')
- grad_gate: float32 [1024, 4608], P('row', 'col')
- grad_up: float32 [1024, 4608], P('row', 'col')
- grad_down: float32 [4608, 1024], P('col', 'row')
Inputs may be any that keep to these rules, and one draw needn't show every extreme that they name: `segments`: within each row the numbers never fall; each of the 3 documents has 1 to 600 tokens, and one has exactly 600.
All inputs are finite; a program needn't handle non-finite values.
Results may differ from a plain program's by a relative error of at most 0.017.
Values may be sent and summed in bfloat16 or wider, within the bound.
A program may use at most 128 MiB of HBM per device.

v0:
```python
import jax
import jax.numpy as jnp
from jax import lax
from jax.sharding import PartitionSpec as P

HEAD_DIM = 64


epsilon = 1e-05
rope_base = 1000000.0


def positions_of(documents):
    length = documents.shape[0]
    places = jnp.arange(length, dtype=jnp.int32)
    starts_here = jnp.concatenate([places[:1] >= 0, documents[1:] != documents[:-1]])
    doc_start = lax.cummax(jnp.where(starts_here, places, 0), axis=0)
    return places - doc_start


def rotary_tables(positions):
    half_dim = HEAD_DIM // 2
    frequency = rope_base ** (-2.0 * jnp.arange(half_dim, dtype=jnp.float32) / HEAD_DIM)
    angles = positions.astype(jnp.float32)[:, None] * frequency[None, :]
    return (jnp.cos(angles)[:, None, :], jnp.sin(angles)[:, None, :])


def rotate(values, cos_table, sin_table):
    half_dim = HEAD_DIM // 2
    first_half, second = (values[..., :half_dim], values[..., half_dim:])
    return jnp.concatenate(
        [first_half * cos_table - second * sin_table, second * cos_table + first_half * sin_table],
        axis=-1,
    )


def rotate_back(gradient, cos_table, sin_table):
    half_dim = HEAD_DIM // 2
    first_half, second = (gradient[..., :half_dim], gradient[..., half_dim:])
    return jnp.concatenate(
        [first_half * cos_table + second * sin_table, second * cos_table - first_half * sin_table],
        axis=-1,
    )


def head_rates(values):
    return lax.rsqrt(jnp.mean(values * values, axis=-1, keepdims=True) + epsilon)


def head_back(values, rate_rows, gain, gradient):
    scaled = gain * gradient
    inner_mean = jnp.mean(scaled * values, axis=-1, keepdims=True)
    return (
        rate_rows * scaled - values * rate_rows**3 * inner_mean,
        jnp.sum(gradient * values * rate_rows, axis=(0, 1)),
    )


def row_total(values):
    return lax.psum(values, "row")


def times_plain(matrix):
    return lambda row_block: jnp.dot(row_block, matrix, preferred_element_type=jnp.float32)


def times_turned(matrix):
    return lambda row_block: lax.dot_general(
        row_block, matrix, (((1,), (1,)), ((), ())), preferred_element_type=jnp.float32
    )


def to_heads(activations, matrix, turned):
    gathered = lax.all_gather(activations, "col", axis=0, tiled=True)
    maker = times_turned if turned else times_plain
    product = maker(matrix)

    def partial_value(offset, amount):
        return product(gathered)

    return (
        gathered,
        lax.psum_scatter(
            partial_value(
                jnp.int32(0), lax.axis_size("row") * (gathered.shape[0] // lax.axis_size("row"))
            ),
            "row",
            scatter_dimension=0,
            tiled=True,
        ),
    )


def to_rows(activations, product):
    gathered = lax.all_gather(activations, "row", axis=0, tiled=True)

    def partial_value(offset, amount):
        return product(gathered)

    return (
        gathered,
        lax.psum_scatter(
            partial_value(
                jnp.int32(0), lax.axis_size("col") * (gathered.shape[0] // lax.axis_size("col"))
            ),
            "col",
            scatter_dimension=0,
            tiled=True,
        ),
    )


def outer_sum(left_side, right_side):
    return lax.dot_general(
        left_side, right_side, (((0,), (0,)), ((), ())), preferred_element_type=jnp.float32
    )


def local(
    hidden_in,
    segments,
    norm_in,
    w_query,
    w_key,
    w_value,
    query_gain,
    key_gain,
    w_out,
    norm_mid,
    w_gate,
    w_up,
    w_down,
    cotangent,
):
    low = jnp.bfloat16
    flt = jnp.float32
    feature_slab = hidden_in.shape[1]
    model_width = feature_slab * lax.axis_size("row")
    q_cols = w_query.shape[1]
    k_cols = w_key.shape[1]
    q_local = q_cols // HEAD_DIM
    kv_local = k_cols // HEAD_DIM
    groups = q_local // kv_local
    ff_local = w_gate.shape[1]
    scale_factor = HEAD_DIM ** (-0.5)
    seq_local, length = segments.shape
    stream = seq_local * length
    own_rows = stream // lax.axis_size("row")
    first_row = lax.axis_index("row") * own_rows
    documents = (segments + length * jnp.arange(seq_local, dtype=jnp.int32)[:, None]).reshape(
        stream
    )
    places = jnp.arange(stream, dtype=jnp.int32)
    own_docs = lax.dynamic_slice_in_dim(documents, first_row, own_rows)
    own_places = first_row + jnp.arange(own_rows, dtype=jnp.int32)
    own_positions = lax.dynamic_slice_in_dim(positions_of(documents), first_row, own_rows)
    allowed = (own_docs[:, None] == documents[None, :]) & (own_places[:, None] >= places[None, :])
    cos_table, sin_table = rotary_tables(own_positions)
    w_joined = jnp.concatenate([w_query, w_key, w_value], axis=1)
    w_pair = jnp.concatenate([w_gate, w_up], axis=1)
    rate_in = lax.rsqrt(row_total(jnp.sum(hidden_in * hidden_in, axis=1)) / model_width + epsilon)[
        :, None
    ]
    normed_in = (hidden_in * rate_in * norm_in).astype(low)
    normed_all, projected = to_heads(normed_in, w_joined, False)
    raw_query = projected[:, :q_cols].reshape(own_rows, q_local, HEAD_DIM)
    raw_key = projected[:, q_cols : q_cols + k_cols].reshape(own_rows, kv_local, HEAD_DIM)
    value_own = projected[:, q_cols + k_cols :].astype(low)
    query_rate = head_rates(raw_query)
    key_rate = head_rates(raw_key)
    query_rot = rotate(raw_query * query_rate * query_gain, cos_table, sin_table).astype(low)
    key_rot = rotate(raw_key * key_rate * key_gain, cos_table, sin_table).astype(low)
    key_all, value_all = (
        lax.all_gather(key_rot.reshape(own_rows, k_cols), "row", axis=0, tiled=True),
        lax.all_gather(value_own, "row", axis=0, tiled=True),
    )
    key_heads = key_all.reshape(stream, kv_local, HEAD_DIM)
    value_heads = value_all.reshape(stream, kv_local, HEAD_DIM)
    query_blocks = query_rot.reshape(own_rows, kv_local, groups, HEAD_DIM)
    scores = (
        jnp.einsum("qkgd,skd->kgqs", query_blocks, key_heads, preferred_element_type=flt)
        * scale_factor
    )
    log_total = jnp.log(jnp.sum(jnp.where(allowed, jnp.exp(scores), 0.0), axis=-1, keepdims=True))
    probability = jnp.where(allowed, jnp.exp(scores - log_total), 0.0)
    mixed = (
        jnp.einsum(
            "kgqs,skd->qkgd", probability.astype(low), value_heads, preferred_element_type=flt
        )
        .reshape(own_rows, q_cols)
        .astype(low)
    )
    mixed_all, attn_part = to_rows(mixed, times_plain(w_out))
    resid = hidden_in + attn_part
    rate_mid = lax.rsqrt(row_total(jnp.sum(resid * resid, axis=1)) / model_width + epsilon)[:, None]
    normed_mid = (resid * rate_mid * norm_mid).astype(low)
    mid_all, gate_up = to_heads(normed_mid, w_pair, False)
    gate_pre = gate_up[:, :ff_local]
    up_pre = gate_up[:, ff_local:]
    sigmoid_gate = jax.nn.sigmoid(gate_pre)
    activated = gate_pre * sigmoid_gate
    swiglu = (activated * up_pre).astype(low)
    swiglu_all, down_part = to_rows(swiglu, times_plain(w_down))
    output = resid + down_part
    cot_low = cotangent.astype(low)
    cot_all, grad_swiglu = to_heads(cot_low, w_down, True)
    grad_down = outer_sum(swiglu_all, cot_all)
    grad_gate_act = (
        grad_swiglu * up_pre * sigmoid_gate * (1.0 + gate_pre * (1.0 - sigmoid_gate))
    ).astype(low)
    grad_up_act = (grad_swiglu * activated).astype(low)
    pair_all, grad_normed_mid = to_rows(
        jnp.concatenate([grad_gate_act, grad_up_act], axis=1), times_turned(w_pair)
    )
    grad_pair = outer_sum(mid_all, pair_all)
    grad_gate = grad_pair[:, :ff_local]
    grad_up = grad_pair[:, ff_local:]
    scaled_mid = norm_mid * grad_normed_mid
    mid_inner = row_total(jnp.sum(scaled_mid * resid, axis=1))[:, None] / model_width
    grad_resid = cotangent + rate_mid * scaled_mid - resid * rate_mid**3 * mid_inner
    gain_mid = jnp.sum(grad_normed_mid * resid * rate_mid, axis=0)
    resid_low = grad_resid.astype(low)
    resid_all, grad_mixed = to_heads(resid_low, w_out, True)
    grad_out = outer_sum(mixed_all, resid_all)
    grad_mixed_heads = grad_mixed.astype(low).reshape(own_rows, kv_local, groups, HEAD_DIM)
    scores_again = (
        jnp.einsum("qkgd,skd->kgqs", query_blocks, key_heads, preferred_element_type=flt)
        * scale_factor
    )
    prob_again = jnp.where(allowed, jnp.exp(scores_again - log_total), 0.0)
    grad_value_act = jnp.einsum(
        "kgqs,qkgd->skd", prob_again.astype(low), grad_mixed_heads, preferred_element_type=flt
    )
    grad_probs = jnp.einsum(
        "qkgd,skd->kgqs", grad_mixed_heads, value_heads, preferred_element_type=flt
    )
    row_inner = jnp.sum(prob_again * grad_probs, axis=-1, keepdims=True)
    grad_scores = (prob_again * (grad_probs - row_inner) * scale_factor).astype(low)
    grad_query_rot = jnp.einsum(
        "kgqs,skd->qkgd", grad_scores, key_heads, preferred_element_type=flt
    ).reshape(own_rows, q_local, HEAD_DIM)
    grad_key_rot = jnp.einsum(
        "kgqs,qkgd->skd", grad_scores, query_blocks, preferred_element_type=flt
    )
    key_own, value_grad_own = (
        lax.psum_scatter(
            grad_key_rot.reshape(stream, k_cols).astype(jnp.bfloat16),
            "row",
            scatter_dimension=0,
            tiled=True,
        ).astype(jnp.float32),
        lax.psum_scatter(
            grad_value_act.reshape(stream, k_cols).astype(jnp.bfloat16),
            "row",
            scatter_dimension=0,
            tiled=True,
        ).astype(jnp.float32),
    )
    grad_raw_query, gain_query = head_back(
        raw_query, query_rate, query_gain, rotate_back(grad_query_rot, cos_table, sin_table)
    )
    grad_raw_key, gain_key = head_back(
        raw_key,
        key_rate,
        key_gain,
        rotate_back(key_own.reshape(own_rows, kv_local, HEAD_DIM), cos_table, sin_table),
    )
    grad_proj = jnp.concatenate(
        [
            grad_raw_query.reshape(own_rows, q_cols),
            grad_raw_key.reshape(own_rows, k_cols),
            value_grad_own,
        ],
        axis=1,
    ).astype(low)
    proj_all, grad_normed_in = to_rows(grad_proj, times_turned(w_joined))
    grad_joined = outer_sum(normed_all, proj_all)
    grad_query = grad_joined[:, :q_cols]
    grad_key = grad_joined[:, q_cols : q_cols + k_cols]
    grad_value = grad_joined[:, q_cols + k_cols :]
    scaled_in = norm_in * grad_normed_in
    in_inner = row_total(jnp.sum(scaled_in * hidden_in, axis=1))[:, None] / model_width
    grad_hidden = grad_resid + rate_in * scaled_in - hidden_in * rate_in**3 * in_inner
    gain_in = jnp.sum(grad_normed_in * hidden_in * rate_in, axis=0)
    block_start = lax.axis_index("row") * feature_slab
    spread_in = lax.dynamic_update_slice(jnp.zeros((model_width,), flt), gain_in, (block_start,))
    spread_mid = lax.dynamic_update_slice(jnp.zeros((model_width,), flt), gain_mid, (block_start,))
    sum_in, sum_mid, gain_query, gain_key = lax.psum(
        (spread_in, spread_mid, gain_query, gain_key), ("dp", "row", "col")
    )
    gain_in = lax.dynamic_slice(sum_in, (block_start,), (feature_slab,))
    gain_mid = lax.dynamic_slice(sum_mid, (block_start,), (feature_slab,))
    grad_query, grad_key, grad_value, grad_out, grad_gate, grad_up, grad_down = (
        lax.psum(grad_query.astype(jnp.bfloat16), "dp").astype(jnp.float32),
        lax.psum(grad_key.astype(jnp.bfloat16), "dp").astype(jnp.float32),
        lax.psum(grad_value.astype(jnp.bfloat16), "dp").astype(jnp.float32),
        lax.psum(grad_out.astype(jnp.bfloat16), "dp").astype(jnp.float32),
        lax.psum(grad_gate.astype(jnp.bfloat16), "dp").astype(jnp.float32),
        lax.psum(grad_up.astype(jnp.bfloat16), "dp").astype(jnp.float32),
        lax.psum(grad_down.astype(jnp.bfloat16), "dp").astype(jnp.float32),
    )
    return (
        output,
        grad_hidden,
        gain_in,
        grad_query,
        grad_key,
        grad_value,
        gain_query,
        gain_key,
        grad_out,
        gain_mid,
        grad_gate,
        grad_up,
        grad_down,
    )


def solution(mesh):
    return jax.shard_map(
        local,
        mesh=mesh,
        in_specs=(
            P(("dp", "col"), "row"),
            P("dp", None),
            P("row"),
            P("row", "col"),
            P("row", "col"),
            P("row", "col"),
            P(),
            P(),
            P("col", "row"),
            P("row"),
            P("row", "col"),
            P("row", "col"),
            P("col", "row"),
            P(("dp", "col"), "row"),
        ),
        out_specs=(
            P(("dp", "col"), "row"),
            P(("dp", "col"), "row"),
            P("row"),
            P("row", "col"),
            P("row", "col"),
            P("row", "col"),
            P(),
            P(),
            P("col", "row"),
            P("row"),
            P("row", "col"),
            P("row", "col"),
            P("col", "row"),
        ),
        check_vma=False,
    )
```

profile of v0, /device:TPU:0, one launch (start us, length us, event | category | flops | bytes accessed | tf_op | source)
XLA Modules:
  0.0 847.7 jit_solution(2587518809301332324)
XLA Ops:
  8.4 13.5 %psum.105 = f32[256]{0:T(256)S(1)} all-reduce(f32[256]{0:T(256)S(1)} %multiply_reduce_fusion.8), channel_id=1, replica_groups=mesh['dp'=2,'row'=4,'col'=4] {'row'}, use_global_device_ids=true, to_apply=%region_1.2 | all-reduce | flops 256 | bytes 2048 | tf_op jit(solution)/shard_map/psum | solution.py:60
  23.5 7.2 all_gather.30
  37.7 38.7 %reduce-scatter.11.cloned.1.call-done = f32[256,512]{1,0:T(8,128)} async-done(((f32[1024,512]{1,0:T(8,128)}), f32[256,512]{1,0:T(8,128)}) %reduce-scatter.11.cloned.1.call-update) | async-done | bytes 524304 | tf_op jit(solution)/shard_map/reduce_scatter | solution.py:83
  77.4 13.8 %all_gather.31 = bf16[1024,128]{1,0:T(8,128)(2,1)S(1)} all-gather(bf16[256,128]{1,0:T(8,128)(2,1)S(1)} %slice.152), channel_id=1, replica_groups=mesh['dp'=2,'row'=4,'col'=4] {'row'}, dimensions={0}, use_global_device_ids=true | all-gather | bytes 327680 | tf_op jit(solution)/shard_map/all_gather | solution.py:175
  93.2 13.8 %all_gather.32 = bf16[1024,128]{0,1:T(8,128)(2,1)S(1)} all-gather(bf16[256,128]{0,1:T(8,128)(2,1)S(1)} %bitcast.167), channel_id=1, replica_groups=mesh['dp'=2,'row'=4,'col'=4] {'row'}, dimensions={0}, use_global_device_ids=true | all-gather | bytes 327680 | tf_op jit(solution)/shard_map/all_gather | solution.py:174
  108.5 2.5 convolution_convert_fusion.4
  111.0 14.9 %all_gather.33 = bf16[1024,256]{0,1:T(8,128)(2,1)S(1)} all-gather(bf16[256,256]{0,1:T(8,128)(2,1)S(1)} %bitcast.171), channel_id=1, replica_groups=mesh['dp'=2,'row'=4,'col'=4] {'row'}, dimensions={0}, use_global_device_ids=true | all-gather | bytes 655360 | tf_op jit(solution)/shard_map/all_gather | solution.py:95
  127.4 7.3 all_gather.36
  134.7 3.1 fusion.64
  137.9 1.9 constant_dynamic-update-slice_fusion.4
  139.8 1.9 constant_dynamic-update-slice_fusion.3
  141.8 10.4 %reduce-scatter.13.cloned.1.call-done = f32[256,256]{1,0:T(8,128)} async-done(((f32[1024,256]{1,0:T(8,128)}), f32[256,256]{1,0:T(8,128)}) %reduce-scatter.13.cloned.1.call-update) | async-done | bytes 262160 | tf_op jit(solution)/shard_map/reduce_scatter | solution.py:102
  153.2 11.8 %psum.106 = f32[256]{0:T(256)S(1)} all-reduce(f32[256]{0:T(256)S(1)} %get-tuple-element.30), channel_id=1, replica_groups=mesh['dp'=2,'row'=4,'col'=4] {'row'}, use_global_device_ids=true, to_apply=%region_10.11 | all-reduce | flops 256 | bytes 2048 | tf_op jit(solution)/shard_map/psum | solution.py:60
  166.2 6.5 all_gather.34
  172.7 6.3 fusion.62
  179.1 60.7 %reduce-scatter.19.cloned.1.call-done = f32[256,1152]{1,0:T(8,128)} async-done(((f32[1024,1152]{1,0:T(8,128)}), f32[256,1152]{1,0:T(8,128)}) %reduce-scatter.19.cloned.1.call-update) | async-done | bytes 1179664 | tf_op jit(solution)/shard_map/reduce_scatter | solution.py:83
  239.8 163.8 %reduce-scatter.15.cloned.1.call-done = f32[256,2304]{1,0:T(8,128)} async-done(((f32[1024,2304]{1,0:T(8,128)}), f32[256,2304]{1,0:T(8,128)}) %reduce-scatter.15.cloned.1.call-update) | async-done | bytes 2359312 | tf_op jit(solution)/shard_map/reduce_scatter | solution.py:83
  403.7 3.5 multiply_convert_fusion.1
  408.9 89.9 %all-gather.6.cloned.1.call-done = bf16[1024,2304]{1,0:T(8,128)(2,1)} async-done(((bf16[256,2304]{1,0:T(8,128)(2,1)}), bf16[1024,2304]{1,0:T(8,128)(2,1)}) %all-gather.6.cloned.1.call-update) | async-done | bytes 4718608 | tf_op jit(solution)/shard_map/all_gather | solution.py:95
  498.8 5.1 fusion.65
  503.9 45.3 %all-gather.4.cloned.1.call-done = bf16[1024,1152]{1,0:T(8,128)(2,1)} async-done(((bf16[256,1152]{1,0:T(8,128)(2,1)}), bf16[1024,1152]{1,0:T(8,128)(2,1)}) %all-gather.4.cloned.1.call-update) | async-done | bytes 2359312 | tf_op jit(solution)/shard_map/all_gather | solution.py:95
  549.2 3.5 fusion.63
  552.8 23.1 %reduce-scatter.21.cloned.1.call-done = f32[256,256]{1,0:T(8,128)} async-done(((f32[1024,256]{1,0:T(8,128)}), f32[256,256]{1,0:T(8,128)}) %reduce-scatter.21.cloned.1.call-update) | async-done | bytes 262160 | tf_op jit(solution)/shard_map/reduce_scatter | solution.py:102
  577.5 11.6 %psum.107 = f32[256]{0:T(256)S(1)} all-reduce(f32[256]{0:T(256)S(1)} %get-tuple-element.14), channel_id=1, replica_groups=mesh['dp'=2,'row'=4,'col'=4] {'row'}, use_global_device_ids=true, to_apply=%region_16.17 | all-reduce | flops 256 | bytes 2048 | tf_op jit(solution)/shard_map/psum | solution.py:60
  589.2 14.7 %reduce-scatter.17.cloned.1.call-done = f32[256,256]{1,0:T(8,128)} async-done(((f32[1024,256]{1,0:T(8,128)}), f32[256,256]{1,0:T(8,128)}) %reduce-scatter.17.cloned.1.call-update) | async-done | bytes 262160 | tf_op jit(solution)/shard_map/reduce_scatter | solution.py:102
  603.8 2.0 fusion.57
  605.9 6.8 all_gather.38
  612.6 2.2 fusion.66
  621.4 5.7 fusion.3
  627.1 15.8 %reduce-scatter.23.cloned.1.call-done = f32[256,256]{1,0:T(8,128)} async-done(((f32[1024,256]{1,0:T(8,128)}), f32[256,256]{1,0:T(8,128)}) %reduce-scatter.23.cloned.1.call-update) | async-done | bytes 262160 | tf_op jit(solution)/shard_map/reduce_scatter | solution.py:83
  646.2 3.6 fusion.67
  649.8 7.9 fusion.20
  657.7 7.8 fusion.17
  667.3 4.6 fusion.19
  671.9 1.8 copy.79
  678.1 2.0 multiply_reduce_fusion.1
  680.1 4.1 reduce-scatter.25.cloned.1.call-done
  686.5 18.8 %reduce-scatter.27.cloned.1.call-done = bf16[256,128]{1,0:T(8,128)(2,1)} async-done(((bf16[1024,128]{1,0:T(8,128)(2,1)}), bf16[256,128]{1,0:T(8,128)(2,1)}) %reduce-scatter.27.cloned.1.call-update) | async-done | bytes 65552 | tf_op jit(solution)/shard_map/reduce_scatter | solution.py:252
  707.1 26.5 %all-gather.8.cloned.1.call-done = bf16[1024,512]{1,0:T(8,128)(2,1)} async-done(((bf16[256,512]{1,0:T(8,128)(2,1)}), bf16[1024,512]{1,0:T(8,128)(2,1)}) %all-gather.8.cloned.1.call-update) | async-done | bytes 1048592 | tf_op jit(solution)/shard_map/all_gather | solution.py:95
  733.6 2.7 fusion.68
  736.6 3.3 convolution_convert_fusion.1
  739.9 4.0 convolution_convert_fusion
  748.3 12.6 %reduce-scatter.29.cloned.1.call-done = f32[256,256]{1,0:T(8,128)} async-done(((f32[1024,256]{1,0:T(8,128)}), f32[256,256]{1,0:T(8,128)}) %reduce-scatter.29.cloned.1.call-update) | async-done | bytes 262160 | tf_op jit(solution)/shard_map/reduce_scatter | solution.py:102
  762.2 39.8 %all-reduce = (f32[1024]{0:T(1024)S(1)}, f32[64]{0:T(128)}, f32[64]{0:T(128)}, f32[1024]{0:T(1024)S(1)}) all-reduce(f32[1024]{0:T(1024)S(1)} %dynamic_update_slice.6, f32[64]{0:T(128)S(1)} %reduce_sum.153, f32[64]{0:T(128)S(1)} %reduce_sum.156, ...), channel_id=1, replica_groups=mesh['dp'=2,'row'=4,'col'=4] {'dp','row','col'}, use_global_device_ids=true, to_apply=%region_27.28 | all-reduce | flops 2176 | bytes 17408 | tf_op jit(solution)/shard_map/psum | solution.py:288
  803.3 10.6 %psum.108 = f32[256]{0:T(256)S(1)} all-reduce(f32[256]{0:T(256)S(1)} %get-tuple-element.16), channel_id=1, replica_groups=mesh['dp'=2,'row'=4,'col'=4] {'row'}, use_global_device_ids=true, to_apply=%region_25.26 | all-reduce | flops 256 | bytes 2048 | tf_op jit(solution)/shard_map/psum | solution.py:60
  815.8 13.7 %all-reduce.4.cloned.1.call-done = (bf16[256,256]{1,0:T(8,128)(2,1)}, bf16[256,128]{1,0:T(8,128)(2,1)}, bf16[256,128]{1,0:T(8,128)(2,1)}, bf16[256,256]{1,0:T(8,...) async-done(((bf16[256,256]{1,0:T(8,128)(2,1)}, bf16[256,128]{1,0:T(8,128)(2,1)}, bf16[256,128]{1,0:T(8,128)(2,1)}, ...) | async-done | bytes 2162704 | tf_op jit(solution)/shard_map/psum | solution.py:294
  835.7 2.2 convert_element_type.130
  837.9 2.2 convert_element_type.131
  (185 shorter events, 57.0 us)
Async XLA Ops:
  7.2 127.5 %copy-start = (bf16[1152,256]{1,0:T(8,128)(2,1)S(1)}, bf16[1152,256]{1,0:T(8,128)(2,1)}, u32[]{:S(2)}) copy-start(bf16[1152,256]{1,0:T(8,128)(2,1)} %param.26) | copy-start | bytes 1769476
  7.2 29.2 %copy-start.19 = (s32[1,1024]{1,0:T(1,128)S(1)}, s32[1,1024]{1,0:T(1,128)}, u32[]{:S(2)}) copy-start(s32[1,1024]{1,0:T(1,128)} %param.15) | copy-start | bytes 12292
  7.2 69.3 %reduce-scatter.11.cloned.1.call-start = ((), (), s32[]{:S(2)}) async-start(), calls=%async_computation.10 | async-start | bytes 2621440 | tf_op jit(solution)/shard_map/reduce_scatter | solution.py:83
  23.5 69.6 %copy-start.28 = (f32[64]{0:T(128)S(1)}, f32[64]{0:T(128)}, u32[]{:S(2)}) copy-start(f32[64]{0:T(128)} %param.21) | copy-start | bytes 772
  33.3 58.0 %copy-start.5 = (bf16[256,512]{1,0:T(8,128)(2,1)}, bf16[256,512]{1,0:T(8,128)(2,1)S(1)}, u32[]{:S(2)}) copy-start(bf16[256,512]{1,0:T(8,128)(2,1)S(1)} %constant_dynamic-update-slice_fusion) | copy-start | bytes 786436
  33.3 75.0 %copy-start.23 = (f32[64]{0:T(128)S(1)}, f32[64]{0:T(128)}, u32[]{:S(2)}) copy-start(f32[64]{0:T(128)} %param.20) | copy-start | bytes 772
  35.1 117.0 %reduce-scatter.13.cloned.1.call-start = ((), (), s32[]{:S(2)}) async-start(), calls=%async_computation.11 | async-start | bytes 1310720 | tf_op jit(solution)/shard_map/reduce_scatter | solution.py:102
  37.7 73.3 %copy-start.15 = (pred[256,1024]{0,1:T(8,128)(4,1)}, pred[256,1024]{0,1:T(8,128)(4,1)S(1)}, u32[]{:S(2)}) copy-start(pred[256,1024]{0,1:T(8,128)(4,1)S(1)} %fusion.24) | copy-start | bytes 786436
  91.3 19.7 %copy-start.6 = (bf16[1024,128]{0,1:T(8,128)(2,1)}, bf16[1024,128]{0,1:T(8,128)(2,1)S(1)}, u32[]{:S(2)}) copy-start(bf16[1024,128]{0,1:T(8,128)(2,1)S(1)} %copy.63) | copy-start | bytes 786436
  92.4 14.6 %copy-start.3 = (f32[256,128]{0,1:T(8,128)}, f32[256,128]{0,1:T(8,128)S(1)}, u32[]{:S(2)}) copy-start(f32[256,128]{0,1:T(8,128)S(1)} %copy.64) | copy-start | bytes 393220
  107.1 4.0 copy-start.14
  108.5 2.6 copy-start.16
  108.5 2.6 copy-start.18
  108.5 17.5 %copy-start.13 = (bf16[256,256]{1,0:T(8,128)(2,1)S(1)}, bf16[256,256]{1,0:T(8,128)(2,1)}, u32[]{:S(2)}) copy-start(bf16[256,256]{1,0:T(8,128)(2,1)} %param.22) | copy-start | bytes 393220
  108.5 18.9 %copy-start.9 = (f32[256,256]{1,0:T(8,128)S(1)}, f32[256,256]{1,0:T(8,128)}, u32[]{:S(2)}) copy-start(f32[256,256]{1,0:T(8,128)} %param.27) | copy-start | bytes 786436
  127.3 112.5 %reduce-scatter.19.cloned.1.call-start = ((), (), s32[]{:S(2)}) async-start(), calls=%async_computation.15 | async-start | bytes 5898240 | tf_op jit(solution)/shard_map/reduce_scatter | solution.py:83
  137.8 14.3 %copy-start.2 = (f32[256,256]{1,0:T(8,128)S(1)}, f32[256,256]{1,0:T(8,128)}, u32[]{:S(2)}) copy-start(f32[256,256]{1,0:T(8,128)} %param.14) | copy-start | bytes 786436
  137.8 28.3 %copy-start.21 = (f32[256]{0:T(256)S(1)}, f32[256]{0:T(256)}, u32[]{:S(2)}) copy-start(f32[256]{0:T(256)} %param.23) | copy-start | bytes 3076
  137.8 265.8 %reduce-scatter.15.cloned.1.call-start = ((), (), s32[]{:S(2)}) async-start(), calls=%async_computation.12 | async-start | bytes 11796480 | tf_op jit(solution)/shard_map/reduce_scatter | solution.py:83
  165.6 0.6 copy-start.20
  179.0 319.7 %all-gather.6.cloned.1.call-start = ((), (), s32[]{:S(2)}) async-start(), calls=%async_computation.16 | async-start | bytes 5898240 | tf_op jit(solution)/shard_map/all_gather | solution.py:95
  408.3 140.9 %all-gather.4.cloned.1.call-start = ((), (), s32[]{:S(2)}) async-start(), calls=%async_computation.13 | async-start | bytes 2949120 | tf_op jit(solution)/shard_map/all_gather | solution.py:95
  408.9 167.0 %reduce-scatter.21.cloned.1.call-start = ((), (), s32[]{:S(2)}) async-start(), calls=%async_computation.17 | async-start | bytes 1310720 | tf_op jit(solution)/shard_map/reduce_scatter | solution.py:102
  503.9 100.0 %reduce-scatter.17.cloned.1.call-start = ((), (), s32[]{:S(2)}) async-start(), calls=%async_computation.14 | async-start | bytes 1310720 | tf_op jit(solution)/shard_map/reduce_scatter | solution.py:102
  552.7 68.7 %copy-start.17 = (bf16[256,4,32]{0,2,1:T(8,128)(2,1)S(1)}, bf16[256,4,32]{0,2,1:T(8,128)(2,1)}, u32[]{:S(2)}) copy-start(bf16[256,4,32]{0,2,1:T(8,128)(2,1)} %copy-done.16) | copy-start | bytes 196612
  552.7 90.2 %reduce-scatter.23.cloned.1.call-start = ((), (), s32[]{:S(2)}) async-start(), calls=%async_computation.18 | async-start | bytes 1310720 | tf_op jit(solution)/shard_map/reduce_scatter | solution.py:83
  614.9 69.3 %reduce-scatter.25.cloned.1.call-start = ((), (), s32[]{:S(2)}) async-start(), calls=%async_computation.19 | async-start | bytes 327680 | tf_op jit(solution)/shard_map/reduce_scatter | solution.py:246
  621.4 24.8 %copy-start.7 = (bf16[1024,128]{0,1:T(8,128)(2,1)S(1)}, bf16[1024,128]{0,1:T(8,128)(2,1)}, u32[]{:S(2)}) copy-start(bf16[1024,128]{0,1:T(8,128)(2,1)} %copy-done.6) | copy-start | bytes 786436
  649.8 17.4 %copy-start.12 = (bf16[256,256]{0,1:T(8,128)(2,1)S(1)}, bf16[256,256]{0,1:T(8,128)(2,1)}, u32[]{:S(2)}) copy-start(bf16[256,256]{0,1:T(8,128)(2,1)} %copy.67) | copy-start | bytes 393220
  665.6 39.8 %reduce-scatter.27.cloned.1.call-start = ((), (), s32[]{:S(2)}) async-start(), calls=%async_computation.20 | async-start | bytes 327680 | tf_op jit(solution)/shard_map/reduce_scatter | solution.py:252
  667.3 6.4 copy-start.24
  667.3 10.8 %copy-start.27 = (f32[256]{0:T(256)S(1)}, f32[256]{0:T(256)}, u32[]{:S(2)}) copy-start(f32[256]{0:T(256)} %mul.498) | copy-start | bytes 3076
  671.9 13.2 %copy-start.4 = (f32[256,128]{0,1:T(8,128)S(1)}, f32[256,128]{0,1:T(8,128)}, u32[]{:S(2)}) copy-start(f32[256,128]{0,1:T(8,128)} %copy-done.3) | copy-start | bytes 393220
  671.9 13.2 %copy-start.29 = (f32[64]{0:T(128)S(1)}, f32[64]{0:T(128)}, u32[]{:S(2)}) copy-start(f32[64]{0:T(128)} %param.21) | copy-start | bytes 772
  678.0 55.6 %all-gather.8.cloned.1.call-start = ((), (), s32[]{:S(2)}) async-start(), calls=%async_computation.21 | async-start | bytes 1310720 | tf_op jit(solution)/shard_map/all_gather | solution.py:95
  707.0 53.8 %reduce-scatter.29.cloned.1.call-start = ((), (), s32[]{:S(2)}) async-start(), calls=%async_computation.22 | async-start | bytes 1310720 | tf_op jit(solution)/shard_map/reduce_scatter | solution.py:102
  736.3 93.1 %all-reduce.4.cloned.1.call-start = ((), (), s32[]{:S(2)}) async-start(), calls=%async_computation.23 | async-start | bytes 4325376 | tf_op jit(solution)/shard_map/psum | solution.py:294
  739.9 6.1 copy-start.8
  743.9 3.9 copy-start.25
  743.9 16.9 %copy-start.22 = (f32[256]{0:T(256)S(1)}, f32[256]{0:T(256)}, u32[]{:S(2)}) copy-start(f32[256]{0:T(256)} %param.16) | copy-start | bytes 3076
  743.9 70.0 %copy-start.10 = (f32[256,256]{1,0:T(8,128)S(1)}, f32[256,256]{1,0:T(8,128)}, u32[]{:S(2)}) copy-start(f32[256,256]{1,0:T(8,128)} %get-tuple-element.29) | copy-start | bytes 786436
  743.9 70.0 %copy-start.26 = (f32[256]{0:T(256)S(1)}, f32[256]{0:T(256)}, u32[]{:S(2)}) copy-start(f32[256]{0:T(256)} %get-tuple-element.62) | copy-start | bytes 3076
  747.8 93.3 %copy-start.1 = (bf16[1152,256]{1,0:T(8,128)(2,1)S(1)}, bf16[1152,256]{1,0:T(8,128)(2,1)}, u32[]{:S(2)}) copy-start(bf16[1152,256]{1,0:T(8,128)(2,1)} %param.26) | copy-start | bytes 1769476
  829.4 10.6 %copy-start.11 = (bf16[1152,256]{1,0:T(8,128)(2,1)S(1)}, bf16[1152,256]{1,0:T(8,128)(2,1)}, u32[]{:S(2)}) copy-start(bf16[1152,256]{1,0:T(8,128)(2,1)} %get-tuple-element.27) | copy-start | bytes 1769476
Sparse Core Ops, SparseCore 0:
  35.3 41.1 reduce-scatter.10
  127.5 24.6 reduce-scatter.12
  154.4 85.3 reduce-scatter.18
  242.0 161.5 reduce-scatter.14
  408.4 90.3 all-gather.5
  500.8 48.3 all-gather.3
  552.3 23.5 reduce-scatter.20
  579.0 24.8 reduce-scatter.16
  615.0 27.8 reduce-scatter.22
  665.7 18.4 reduce-scatter.24
  687.1 18.2 reduce-scatter.26
  707.3 26.2 all-gather.7
  736.7 24.1 reduce-scatter.28
  764.6 64.7 all-reduce.3
where the time goes:
time: 849 us; the launch traced here: 848 us
  waiting for transfers between devices  539 us (63%)
  blocking collectives  158 us (19%)
  matrix products  66.8 us (8%)
  other arithmetic  40.1 us (5%)
  local copies, waits for them, and re-layouts  28.4 us (3%)
  between operations  15.2 us (2%)
    reduce_scatter x4, waiting for transfers between devices, to_heads(): lax.psum_scatter(partial_value(jnp.int32(0), lax.axis_size('row') * (gath...  279 us
    all_gather x3, waiting for transfers between devices, to_rows(): gathered = lax.all_gather(activations, 'row', axis=0, tiled=True)  162 us
    reduce_scatter x4, waiting for transfers between devices, to_rows(): lax.psum_scatter(partial_value(jnp.int32(0), lax.axis_size('col') * (gath...  60.7 us
    psum x4, blocking collectives, row_total(): return lax.psum(values, 'row')  47.6 us
    psum x1, blocking collectives, local(): lax.psum((spread_in, spread_mid, gain_query, gain_key), ('dp', 'row', 'co...  39.8 us
    all_gather x4, blocking collectives, to_heads(): gathered = lax.all_gather(activations, 'col', axis=0, tiled=True)  27.7 us
    reduce_scatter x1, waiting for transfers between devices, local(): lax.psum_scatter(grad_value_act.reshape(stream, k_cols).astype(jnp.bfloat...  18.8 us
  transfers between devices with their start and end apart: 14, of which 14 were waited for; matrix products, arithmetic and copies ran while one was open for 8% of the time, Pallas kernels for 0%

commit v1 on v0

v1 whole, which is shorter than its diff:
```python
import functools

import jax
import jax.numpy as jnp
from jax import lax
from jax.experimental import pallas as pl
from jax.experimental.pallas import tpu as pltpu
from jax.sharding import PartitionSpec as P

HEAD_DIM = 64


epsilon = 1e-05
rope_base = 1000000.0


def positions_of(documents):
    length = documents.shape[0]
    places = jnp.arange(length, dtype=jnp.int32)
    starts_here = jnp.concatenate([places[:1] >= 0, documents[1:] != documents[:-1]])
    doc_start = lax.cummax(jnp.where(starts_here, places, 0), axis=0)
    return places - doc_start


def rotary_tables(positions):
    half_dim = HEAD_DIM // 2
    frequency = rope_base ** (-2.0 * jnp.arange(half_dim, dtype=jnp.float32) / HEAD_DIM)
    angles = positions.astype(jnp.float32)[:, None] * frequency[None, :]
    return (jnp.cos(angles)[:, None, :], jnp.sin(angles)[:, None, :])


def rotate(values, cos_table, sin_table):
    half_dim = HEAD_DIM // 2
    first_half, second = (values[..., :half_dim], values[..., half_dim:])
    return jnp.concatenate(
        [first_half * cos_table - second * sin_table, second * cos_table + first_half * sin_table],
        axis=-1,
    )


def rotate_back(gradient, cos_table, sin_table):
    half_dim = HEAD_DIM // 2
    first_half, second = (gradient[..., :half_dim], gradient[..., half_dim:])
    return jnp.concatenate(
        [first_half * cos_table + second * sin_table, second * cos_table - first_half * sin_table],
        axis=-1,
    )


def head_rates(values):
    return lax.rsqrt(jnp.mean(values * values, axis=-1, keepdims=True) + epsilon)


def head_back(values, rate_rows, gain, gradient):
    scaled = gain * gradient
    inner_mean = jnp.mean(scaled * values, axis=-1, keepdims=True)
    return (
        rate_rows * scaled - values * rate_rows**3 * inner_mean,
        jnp.sum(gradient * values * rate_rows, axis=(0, 1)),
    )


def part(ref, dim, index, size):
    if dim is None:
        return ref
    if dim == "lead":
        return ref.at[index]
    start = pl.multiple_of(index * size, size)
    return ref.at[(slice(None),) * dim + (pl.ds(start, size),)]


def swap_kernel(ops, sizes, *refs):
    count = len(ops)
    ins, outs = refs[:count], refs[count : 2 * count]
    send_sem, recv_sem, own_sem = refs[2 * count :]
    axes = sorted({op[0] for op in ops})
    me = {axis: lax.axis_index(axis) for axis in axes}
    barrier = pltpu.get_barrier_semaphore()
    for axis in axes:
        for step in range(1, sizes[axis]):
            pl.semaphore_signal(
                barrier,
                inc=1,
                device_id={axis: lax.rem(me[axis] + step, sizes[axis])},
                device_id_type=pl.DeviceIdType.MESH,
            )
    pl.semaphore_wait(barrier, sum(sizes[axis] - 1 for axis in axes))
    copies = []
    slot = 0
    for place, (axis, src_dim, src_size, dst_dim, dst_size) in enumerate(ops):
        for step in range(1, sizes[axis]):
            peer = lax.rem(me[axis] + step, sizes[axis])
            copy = pltpu.make_async_remote_copy(
                src_ref=part(ins[place], src_dim, peer, src_size),
                dst_ref=part(outs[place], dst_dim, me[axis], dst_size),
                send_sem=send_sem.at[slot],
                recv_sem=recv_sem.at[slot],
                device_id={axis: peer},
                device_id_type=pl.DeviceIdType.MESH,
            )
            copy.start()
            copies.append(copy)
            slot += 1
    for place, (axis, src_dim, src_size, dst_dim, dst_size) in enumerate(ops):
        copy = pltpu.make_async_copy(
            part(ins[place], src_dim, me[axis], src_size),
            part(outs[place], dst_dim, me[axis], dst_size),
            own_sem.at[place],
        )
        copy.start()
        copies.append(copy)
    for copy in copies:
        copy.wait()


def swap(ident, *ops):
    sizes = {op[0]: lax.axis_size(op[0]) for op in ops}
    plans, shapes = [], []
    for axis, array, src_dim, dst_dim in ops:
        n = sizes[axis]
        block = list(array.shape)
        src_size = dst_size = None
        if src_dim == "lead":
            block = block[1:]
        elif src_dim is not None:
            block[src_dim] //= n
            src_size = block[src_dim]
        if dst_dim == "lead":
            block = [n] + block
        else:
            dst_size = block[dst_dim]
            block[dst_dim] *= n
        plans.append((axis, src_dim, src_size, dst_dim, dst_size))
        shapes.append(jax.ShapeDtypeStruct(tuple(block), array.dtype))
    slots = sum(sizes[op[0]] - 1 for op in ops)
    return pl.pallas_call(
        functools.partial(swap_kernel, tuple(plans), sizes),
        out_shape=tuple(shapes),
        in_specs=[pl.BlockSpec(memory_space=pltpu.VMEM)] * len(ops),
        out_specs=(pl.BlockSpec(memory_space=pltpu.VMEM),) * len(ops),
        scratch_shapes=[
            pltpu.SemaphoreType.DMA((slots,)),
            pltpu.SemaphoreType.DMA((slots,)),
            pltpu.SemaphoreType.DMA((len(ops),)),
        ],
        compiler_params=pltpu.CompilerParams(collective_id=ident, has_side_effects=True),
    )(*[op[1] for op in ops])


def dot(left_side, right_side):
    return jnp.dot(left_side, right_side, preferred_element_type=jnp.float32)


def dot_turned(left_side, right_side):
    return lax.dot_general(
        left_side, right_side, (((1,), (1,)), ((), ())), preferred_element_type=jnp.float32
    )


def outer_sum(left_side, right_side):
    return lax.dot_general(
        left_side, right_side, (((0,), (0,)), ((), ())), preferred_element_type=jnp.float32
    )


def eight(vector):
    return jnp.broadcast_to(vector[None, :], (8,) + vector.shape)


def added(stacked):
    return jnp.sum(stacked.astype(jnp.float32), axis=0)


def local(
    hidden_in,
    segments,
    norm_in,
    w_query,
    w_key,
    w_value,
    query_gain,
    key_gain,
    w_out,
    norm_mid,
    w_gate,
    w_up,
    w_down,
    cotangent,
):
    low = jnp.bfloat16
    flt = jnp.float32
    rows = lax.axis_size("row")
    slab_rows, feature_slab = hidden_in.shape
    model_width = feature_slab * rows
    q_cols = w_query.shape[1]
    k_cols = w_key.shape[1]
    q_mine = q_cols // HEAD_DIM // rows
    kv_local = k_cols // HEAD_DIM
    kv_mine = max(1, kv_local // rows)
    share = rows * kv_mine // kv_local
    groups = q_mine // kv_mine
    q_width, k_width = q_mine * HEAD_DIM, kv_mine * HEAD_DIM
    ff_local = w_gate.shape[1]
    ff_mine = ff_local // rows
    scale_factor = HEAD_DIM ** (-0.5)
    seq_local, length = segments.shape
    stream = seq_local * length
    documents = (segments + length * jnp.arange(seq_local, dtype=jnp.int32)[:, None]).reshape(
        stream
    )
    places = jnp.arange(stream, dtype=jnp.int32)
    allowed = (documents[:, None] == documents[None, :]) & (places[:, None] >= places[None, :])
    cos_table, sin_table = rotary_tables(positions_of(documents))

    cot_low = cotangent.astype(low)
    cot_all = lax.all_gather(
        lax.all_gather(cot_low, "row", axis=1, tiled=True), "col", axis=0, tiled=True
    )

    w_joined_parts = jnp.stack(
        [
            jnp.concatenate(
                [
                    w_query[:, r * q_width : (r + 1) * q_width],
                    w_key[:, (r // share) * k_width : (r // share + 1) * k_width],
                    w_value[:, (r // share) * k_width : (r // share + 1) * k_width],
                ],
                axis=1,
            )
            for r in range(rows)
        ]
    )
    w_pair_parts = jnp.stack(
        [
            jnp.stack([w[:, r * ff_mine : (r + 1) * ff_mine] for w in (w_gate, w_up)])
            for r in range(rows)
        ]
    )
    hidden_row, square_in, norm_in_all, norm_mid_all, w_joined, w_out_mine = swap(
        0,
        ("row", hidden_in.astype(low), None, 1),
        ("row", eight(jnp.sum(hidden_in * hidden_in, axis=1)), None, "lead"),
        ("row", eight(norm_in), None, 1),
        ("row", eight(norm_mid), None, 1),
        ("row", w_joined_parts, "lead", 0),
        ("row", w_out, 0, 1),
    )
    rate_in = lax.rsqrt(jnp.sum(square_in, axis=0)[0] / model_width + epsilon)[:, None]
    normed_in, w_pair = swap(
        1,
        ("col", (hidden_row.astype(flt) * rate_in * norm_in_all[:1]).astype(low), None, 0),
        ("row", w_pair_parts, "lead", 1),
    )
    projected = dot(normed_in, w_joined)
    raw_query = projected[:, :q_width].reshape(stream, q_mine, HEAD_DIM)
    raw_key = projected[:, q_width : q_width + k_width].reshape(stream, kv_mine, HEAD_DIM)
    value_heads = projected[:, q_width + k_width :].astype(low).reshape(stream, kv_mine, HEAD_DIM)
    query_rate = head_rates(raw_query)
    key_rate = head_rates(raw_key)
    query_rot = rotate(raw_query * query_rate * query_gain, cos_table, sin_table).astype(low)
    key_heads = rotate(raw_key * key_rate * key_gain, cos_table, sin_table).astype(low)
    query_blocks = query_rot.reshape(stream, kv_mine, groups, HEAD_DIM)
    scores = (
        jnp.einsum("qkgd,skd->kgqs", query_blocks, key_heads, preferred_element_type=flt)
        * scale_factor
    )
    log_total = jnp.log(jnp.sum(jnp.where(allowed, jnp.exp(scores), 0.0), axis=-1, keepdims=True))
    probability = jnp.where(allowed, jnp.exp(scores - log_total), 0.0)
    mixed = (
        jnp.einsum(
            "kgqs,skd->qkgd", probability.astype(low), value_heads, preferred_element_type=flt
        )
        .reshape(stream, q_width)
        .astype(low)
    )
    out_parts, w_down_mine = swap(
        2,
        ("col", dot(mixed, w_out_mine).astype(low), 0, "lead"),
        ("row", w_down, 0, 1),
    )
    (out_cols,) = swap(3, ("row", added(out_parts).astype(low), 1, "lead"))
    resid = hidden_in + added(out_cols)
    resid_row, square_mid = swap(
        4,
        ("row", resid.astype(low), None, 1),
        ("row", eight(jnp.sum(resid * resid, axis=1)), None, "lead"),
    )
    rate_mid = lax.rsqrt(jnp.sum(square_mid, axis=0)[0] / model_width + epsilon)[:, None]
    (normed_mid,) = swap(
        5, ("col", (resid_row.astype(flt) * rate_mid * norm_mid_all[:1]).astype(low), None, 0)
    )
    gate_pre = dot(normed_mid, w_pair[0])
    up_pre = dot(normed_mid, w_pair[1])
    sigmoid_gate = jax.nn.sigmoid(gate_pre)
    activated = gate_pre * sigmoid_gate
    swiglu = (activated * up_pre).astype(low)
    down_part = dot(swiglu, w_down_mine).astype(low)
    down_own = lax.psum_scatter(
        lax.psum_scatter(down_part, "col", scatter_dimension=0, tiled=True),
        "row",
        scatter_dimension=1,
        tiled=True,
    )
    output = resid + down_own.astype(flt)
    grad_swiglu = dot_turned(cot_all, w_down_mine)
    grad_down = outer_sum(swiglu, cot_all).astype(low)
    grad_gate_act = (
        grad_swiglu * up_pre * sigmoid_gate * (1.0 + gate_pre * (1.0 - sigmoid_gate))
    ).astype(low)
    grad_up_act = (grad_swiglu * activated).astype(low)
    mid_part = dot_turned(grad_gate_act, w_pair[0]) + dot_turned(grad_up_act, w_pair[1])
    grad_gate = outer_sum(normed_mid, grad_gate_act).astype(low)
    grad_up = outer_sum(normed_mid, grad_up_act).astype(low)
    mid_parts, grad_gate_got, grad_up_got = swap(
        6,
        ("col", mid_part.astype(low), 0, "lead"),
        ("row", grad_gate, 0, "lead"),
        ("row", grad_up, 0, "lead"),
    )
    (mid_cols,) = swap(7, ("row", added(mid_parts).astype(low), 1, "lead"))
    grad_normed_mid = added(mid_cols)
    scaled_mid = norm_mid * grad_normed_mid
    first_mid = cotangent + rate_mid * scaled_mid
    first_row, inner_got = swap(
        8,
        ("row", first_mid.astype(low), None, 1),
        ("row", eight(jnp.sum(scaled_mid * resid, axis=1)), None, "lead"),
    )
    mid_scale = rate_mid**3 * (jnp.sum(inner_got, axis=0)[0][:, None] / model_width)
    grad_resid = first_mid - resid * mid_scale
    gain_mid = jnp.sum(grad_normed_mid * resid * rate_mid, axis=0)
    resid_low, grad_down_got = swap(
        9,
        ("col", (first_row.astype(flt) - resid_row.astype(flt) * mid_scale).astype(low), None, 0),
        ("row", grad_down, 1, 0),
    )

    def unfold(got):
        return jnp.moveaxis(got, 0, 1).reshape(got.shape[1], -1)

    grad_gate, grad_up, grad_down = (
        value.astype(flt)
        for value in lax.psum((unfold(grad_gate_got), unfold(grad_up_got), grad_down_got), "dp")
    )
    grad_out = outer_sum(mixed, resid_low).astype(low)
    grad_mixed_heads = (
        dot_turned(resid_low, w_out_mine).astype(low).reshape(stream, kv_mine, groups, HEAD_DIM)
    )
    grad_value_act = jnp.einsum(
        "kgqs,qkgd->skd", probability.astype(low), grad_mixed_heads, preferred_element_type=flt
    )
    grad_probs = jnp.einsum(
        "qkgd,skd->kgqs", grad_mixed_heads, value_heads, preferred_element_type=flt
    )
    row_inner = jnp.sum(probability * grad_probs, axis=-1, keepdims=True)
    grad_scores = (probability * (grad_probs - row_inner) * scale_factor).astype(low)
    grad_query_rot = jnp.einsum(
        "kgqs,skd->qkgd", grad_scores, key_heads, preferred_element_type=flt
    ).reshape(stream, q_mine, HEAD_DIM)
    grad_key_rot = jnp.einsum(
        "kgqs,qkgd->skd", grad_scores, query_blocks, preferred_element_type=flt
    )
    grad_raw_query, gain_query = head_back(
        raw_query, query_rate, query_gain, rotate_back(grad_query_rot, cos_table, sin_table)
    )
    grad_raw_key, gain_key = head_back(
        raw_key, key_rate, key_gain, rotate_back(grad_key_rot, cos_table, sin_table)
    )
    grad_proj = jnp.concatenate(
        [
            grad_raw_query.reshape(stream, q_width),
            grad_raw_key.reshape(stream, k_width),
            grad_value_act.reshape(stream, k_width),
        ],
        axis=1,
    ).astype(low)
    grad_joined = outer_sum(normed_in, grad_proj).astype(low)
    in_parts, joined_got, out_got = swap(
        10,
        ("col", dot_turned(grad_proj, w_joined).astype(low), 0, "lead"),
        ("row", grad_joined, 0, "lead"),
        ("row", grad_out, 1, 0),
    )
    (in_cols,) = swap(11, ("row", added(in_parts).astype(low), 1, "lead"))
    grad_normed_in = added(in_cols)
    scaled_in = norm_in * grad_normed_in
    (in_inner,) = swap(12, ("row", eight(jnp.sum(scaled_in * hidden_in, axis=1)), None, "lead"))
    in_scale = rate_in**3 * (jnp.sum(in_inner, axis=0)[0][:, None] / model_width)
    grad_hidden = grad_resid + rate_in * scaled_in - hidden_in * in_scale
    gain_in = jnp.sum(grad_normed_in * hidden_in * rate_in, axis=0)

    def shared(got):
        summed = got.astype(flt).reshape(rows // share, share, feature_slab, k_width).sum(axis=1)
        return unfold(summed).astype(low)

    grad_query, grad_key, grad_value, grad_out = (
        value.astype(flt)
        for value in lax.psum(
            (
                unfold(joined_got[:, :, :q_width]),
                shared(joined_got[:, :, q_width : q_width + k_width]),
                shared(joined_got[:, :, q_width + k_width :]),
                out_got,
            ),
            "dp",
        )
    )
    block_start = lax.axis_index("row") * feature_slab
    spread_in = lax.dynamic_update_slice(jnp.zeros((model_width,), flt), gain_in, (block_start,))
    spread_mid = lax.dynamic_update_slice(jnp.zeros((model_width,), flt), gain_mid, (block_start,))
    sum_in, sum_mid, gain_query, gain_key = lax.psum(
        (spread_in, spread_mid, gain_query, gain_key), ("dp", "row", "col")
    )
    gain_in = lax.dynamic_slice(sum_in, (block_start,), (feature_slab,))
    gain_mid = lax.dynamic_slice(sum_mid, (block_start,), (feature_slab,))
    return (
        output,
        grad_hidden,
        gain_in,
        grad_query,
        grad_key,
        grad_value,
        gain_query,
        gain_key,
        grad_out,
        gain_mid,
        grad_gate,
        grad_up,
        grad_down,
    )


def solution(mesh):
    return jax.shard_map(
        local,
        mesh=mesh,
        in_specs=(
            P(("dp", "col"), "row"),
            P("dp", None),
            P("row"),
            P("row", "col"),
            P("row", "col"),
            P("row", "col"),
            P(),
            P(),
            P("col", "row"),
            P("row"),
            P("row", "col"),
            P("row", "col"),
            P("col", "row"),
            P(("dp", "col"), "row"),
        ),
        out_specs=(
            P(("dp", "col"), "row"),
            P(("dp", "col"), "row"),
            P("row"),
            P("row", "col"),
            P("row", "col"),
            P("row", "col"),
            P(),
            P(),
            P("col", "row"),
            P("row"),
            P("row", "col"),
            P("row", "col"),
            P("col", "row"),
        ),
        check_vma=False,
    )
```

time: 849 us -> 523 us (0.62)
  waiting for transfers between devices: 539 us -> 9.19 us
  Pallas kernels: 0 us -> 314 us
  blocking collectives: 158 us -> 60.1 us
  matrix products: 66.8 us -> 49.2 us
    reduce_scatter x10 -> x2, waiting for transfers between devices: 363 us -> 8.64 us  [the longest x1 8.62 us: local(): lax.psum_scatter(lax.psum_scatter(down_part, 'col', scatter_dimension=0,...]
    pallas_call x0 -> x13, Pallas kernels: none -> 314 us  [swap(): pl.pallas_call(functools.partial(swap_kernel, tuple(plans), sizes), out_s...]
    all_gather x3 -> x1, waiting for transfers between devices: 162 us -> 0.01 us  [local(): lax.all_gather(lax.all_gather(cot_low, 'row', axis=1, tiled=True), 'col',...]
    all_gather x7 -> x1, blocking collectives: 70.3 us -> 18 us  [local(): lax.all_gather(cot_low, 'row', axis=1, tiled=True)]
    psum x4 -> x0, blocking collectives: 47.6 us -> none  [row_total(): return lax.psum(values, 'row')]
    reduce_sum x0 -> x11, other arithmetic: none -> 14.8 us  [the longest x6 10.6 us: added(): return jnp.sum(stacked.astype(jnp.float32), axis=0)]
    psum x1, waiting for transfers between devices: 13.7 us -> 0.02 us  [local(): lax.psum((unfold(joined_got[:, :, :q_width]), shared(joined_got[:, :, q_w...]
    convert_element_type x12 -> x6, other arithmetic: 20 us -> 8.45 us  [the longest x2 2.72 us: local(): value.astype(flt)]
  transfers between devices with their start and end apart: 14 -> 4, of which waited for: 14 -> 1; matrix products, arithmetic and copies ran while one was open for 8% -> 19% of each run, Pallas kernels for 0% -> 60%
where the time goes in v1:
time: 523 us; the launch traced here: 521 us
  Pallas kernels  314 us (60%)
  blocking collectives  60.1 us (11%)
  matrix products  49.2 us (9%)
  other arithmetic  38.5 us (7%)
  local copies, waits for them, and re-layouts  34.7 us (7%)
  between operations  15.3 us (3%)
  waiting for transfers between devices  9.19 us (2%)
    pallas_call x13, Pallas kernels, swap(): pl.pallas_call(functools.partial(swap_kernel, tuple(plans), sizes), out_s...  314 us
    psum x1, blocking collectives, local(): lax.psum((spread_in, spread_mid, gain_query, gain_key), ('dp', 'row', 'co...  42.1 us
    all_gather x1, blocking collectives, local(): lax.all_gather(cot_low, 'row', axis=1, tiled=True)  18 us
    dot_general x5, matrix products, dot_turned(): lax.dot_general(left_side, right_side, (((1,), (1,)), ((), ())), preferre...  17.2 us
    dot_general x5, matrix products, dot(): return jnp.dot(left_side, right_side, preferred_element_type=jnp.float32)  14.1 us
    unnamed x131, local copies, waits for them, and re-layouts  10.7 us
    reduce_sum x6, other arithmetic, added(): return jnp.sum(stacked.astype(jnp.float32), axis=0)  10.6 us
  transfers between devices with their start and end apart: 4, of which 1 were waited for; matrix products, arithmetic and copies ran while one was open for 19% of the time, Pallas kernels for 60%

profile of v1, /device:TPU:0, one launch (start us, length us, event | category | flops | bytes accessed | tf_op | source)
XLA Modules:
  0.0 520.9 jit_solution(652729264403287245)
XLA Ops:
  8.3 18.0 %all_gather.6 = bf16[256,1024]{1,0:T(8,128)(2,1)} all-gather(bf16[256,256]{1,0:T(8,128)(2,1)S(1)} %convert_element_type.185), channel_id=1, replica_groups=mesh['dp'=2,'row'=4,'col'=4] {'row'}, dimensions={1}, use_global_device_ids=true | all-gather | bytes 655360 | tf_op jit(solution)/shard_map/all_gather | solution.py:217
  34.8 31.4 %shard_map.240 = (bf16[256,1024]{1,0:T(8,128)(2,1)}, f32[4,8,256]{2,1,0:T(8,128)}, f32[8,1024]{1,0:T(8,128)}, f32[8,1024]{1,0:T(8,128)}, bf16[1024,192]{1,0:T(8,128)(2,1)}, /*index=5*/bf16[64,1024]{1,0:T(8,128)(2,1)}) custom-call(bf16[256,256]{1,0:T(8,128)(2,1)} %get-tuple-element.150.refs_0_, f32[8,256]{1,0:T(8,128)} %broadcast_in_dim.22.refs_1_, ...), custom_call_target="tpu_custom_call" | custom-call | tf_op jit(solution)/shard_map/pallas_call | solution.py:136
  67.1 1.4 slice.170
  71.2 1.5 pad_maximum_fusion.refs_1_
  72.7 33.3 %shard_map.241 = (bf16[1024,1024]{1,0:T(8,128)(2,1)}, bf16[2,1024,288]{2,1,0:T(8,128)(2,1)}) custom-call(bf16[256,1024]{1,0:T(8,128)(2,1)} %multiply_convert_fusion.3.refs_0_, bf16[4,2,256,288]{3,2,1,0:T(8,128)(2,1)} %pad_maximum_fusion.refs_1_), custom_call_target="tpu_custom_call" | custom-call | tf_op jit(solution)/shard_map/pallas_call | solution.py:136
  106.1 2.4 fusion.105
  113.6 2.1 convolution_convert_fusion.2.refs_0_
  115.6 34.6 %shard_map.242 = (bf16[4,256,1024]{2,1,0:T(8,128)(2,1)}, bf16[288,1024]{1,0:T(8,128)(2,1)}) custom-call(bf16[1024,1024]{1,0:T(8,128)(2,1)} %convolution_convert_fusion.2.refs_0_, bf16[1152,256]{1,0:T(8,128)(2,1)} %refs_1_.1), custom_call_target="tpu_custom_call" | custom-call | tf_op jit(solution)/shard_map/pallas_call | solution.py:136
  150.3 2.9 reduce_sum.248.refs_0_
  153.2 14.5 %shard_map.243 = bf16[4,256,256]{2,1,0:T(8,128)(2,1)} custom-call(bf16[256,1024]{1,0:T(8,128)(2,1)} %reduce_sum.248.refs_0_), custom_call_target="tpu_custom_call" | custom-call | tf_op jit(solution)/shard_map/pallas_call | solution.py:136
  170.3 19.7 %shard_map.244 = (bf16[256,1024]{1,0:T(8,128)(2,1)}, f32[4,8,256]{2,1,0:T(8,128)}) custom-call(bf16[256,256]{1,0:T(8,128)(2,1)} %convert_element_type.179.refs_0_, f32[8,256]{1,0:T(8,128)} %broadcast_in_dim.29.refs_1_), custom_call_target="tpu_custom_call" | custom-call | tf_op jit(solution)/shard_map/pallas_call | solution.py:136
  190.8 2.0 fusion.27.refs_0_
  192.8 26.9 %shard_map.245 = bf16[1024,1024]{1,0:T(8,128)(2,1)} custom-call(bf16[256,1024]{1,0:T(8,128)(2,1)} %fusion.27.refs_0_), custom_call_target="tpu_custom_call" | custom-call | tf_op jit(solution)/shard_map/pallas_call | solution.py:136
  219.7 3.8 fusion.31
  223.5 1.9 fusion.35
  225.3 4.5 multiply_convert_fusion
  229.8 1.6 convolution_convert_fusion.4
  231.4 3.3 fusion.33
  234.7 1.6 convolution_convert_fusion.3
  236.3 2.2 copy.54.refs_1_
  238.6 2.2 copy.55.refs_2_
  240.8 4.0 convolution_convert_fusion.1
  244.9 5.0 add_convert_fusion.refs_0_
  249.8 41.0 %shard_map.246 = (bf16[4,256,1024]{2,1,0:T(8,128)(2,1)}, bf16[4,256,288]{2,1,0:T(8,128)(2,1)}, bf16[4,256,288]{2,1,0:T(8,128)(2,1)}) custom-call(bf16[1024,1024]{1,0:T(8,128)(2,1)} %add_convert_fusion.refs_0_, bf16[1024,288]{1,0:T(8,128)(2,1)} %copy.54.refs_1_, bf16[1024,288]{1,0:T(8,128)(2,1)} %copy.55.refs_2_), custom_call_target="tpu_custom_call" | custom-call | tf_op jit(solution)/shard_map/pallas_call | solution.py:136
  290.8 2.9 reduce_sum.252.refs_0_
  293.8 16.0 %shard_map.247 = bf16[4,256,256]{2,1,0:T(8,128)(2,1)} custom-call(bf16[256,1024]{1,0:T(8,128)(2,1)} %reduce_sum.252.refs_0_), custom_call_target="tpu_custom_call" | custom-call | tf_op jit(solution)/shard_map/pallas_call | solution.py:136
  310.9 2.3 copy.60
  315.1 18.4 %shard_map.248 = (bf16[256,1024]{1,0:T(8,128)(2,1)}, f32[4,8,256]{2,1,0:T(8,128)}) custom-call(bf16[256,256]{1,0:T(8,128)(2,1)} %get-tuple-element.146.refs_0_, f32[8,256]{1,0:T(8,128)} %broadcast_in_dim.30.refs_1_), custom_call_target="tpu_custom_call" | custom-call | tf_op jit(solution)/shard_map/pallas_call | solution.py:136
  335.4 2.0 fusion.29.refs_0_
  337.5 3.4 convolution_convert_fusion.5.refs_1_
  340.9 27.1 %shard_map.249 = (bf16[1024,1024]{1,0:T(8,128)(2,1)}, bf16[1152,256]{1,0:T(8,128)(2,1)}) custom-call(bf16[256,1024]{1,0:T(8,128)(2,1)} %fusion.29.refs_0_, bf16[288,1024]{1,0:T(8,128)(2,1)} %convolution_convert_fusion.5.refs_1_), custom_call_target="tpu_custom_call" | custom-call | tf_op jit(solution)/shard_map/pallas_call | solution.py:136
  368.0 2.3 convolution_convert_fusion.8
  370.3 3.8 fusion
  374.2 2.4 fusion.7
  379.4 2.0 fusion.20
  383.4 2.0 copy.56.refs_1_
  386.6 2.1 convolution_convert_fusion.refs_0_
  388.7 29.4 %shard_map.250 = (bf16[4,256,1024]{2,1,0:T(8,128)(2,1)}, bf16[4,256,192]{2,1,0:T(8,128)(2,1)}, bf16[256,256]{1,0:T(8,128)(2,1)}) custom-call(bf16[1024,1024]{1,0:T(8,128)(2,1)} %convolution_convert_fusion.refs_0_, bf16[1024,192]{1,0:T(8,128)(2,1)} %copy.56.refs_1_, bf16[64,1024]{1,0:T(8,128)(2,1)} %convolution_convert_fusion.7.refs_2_), custom_call_target="tpu_custom_call" | custom-call | tf_op jit(solution)/shard_map/pallas_call | solution.py:136
  424.5 14.5 %shard_map.251 = bf16[4,256,256]{2,1,0:T(8,128)(2,1)} custom-call(bf16[256,1024]{1,0:T(8,128)(2,1)} %reduce_sum.259.refs_0_), custom_call_target="tpu_custom_call" | custom-call | tf_op jit(solution)/shard_map/pallas_call | solution.py:136
  440.9 42.1 %all-reduce = (f32[1024]{0:T(1024)S(1)}, f32[64]{0:T(128)}, f32[64]{0:T(128)}, f32[1024]{0:T(1024)S(1)}) all-reduce(f32[1024]{0:T(1024)S(1)} %dynamic_update_slice.6, f32[64]{0:T(128)S(1)} %copy-done.60, f32[64]{0:T(128)S(1)} %get-tuple-element.96, ...), channel_id=1, replica_groups=mesh['dp'=2,'row'=4,'col'=4] {'dp','row','col'}, use_global_device_ids=true, to_apply=%region_25.26 | all-reduce | flops 2176 | bytes 17408 | tf_op jit(solution)/shard_map/psum | solution.py:411
  484.9 6.8 %shard_map.252 = f32[4,8,256]{2,1,0:T(8,128)} custom-call(f32[8,256]{1,0:T(8,128)} %broadcast_in_dim.31.refs_0_), custom_call_target="tpu_custom_call" | custom-call | tf_op jit(solution)/shard_map/pallas_call | solution.py:136
  492.5 1.8 copy.62
  494.3 1.6 copy.63
  495.9 1.7 copy.64
  497.6 1.6 convert_element_type.211
  499.2 2.3 copy.65
  503.9 8.6 %reduce-scatter.5.cloned.1.call-done = bf16[256,256]{1,0:T(8,128)(2,1)} async-done(((bf16[256,1024]{1,0:T(8,128)(2,1)}), bf16[256,256]{1,0:T(8,128)(2,1)}) %reduce-scatter.5.cloned.1.call-update) | async-done | bytes 131088 | tf_op jit(solution)/shard_map/reduce_scatter | solution.py:298
  512.5 1.8 multiply_subtract_fusion
  (215 shorter events, 44.7 us)
Async XLA Ops:
  7.2 23.9 %copy-start.7 = (f32[256,256]{1,0:T(8,128)S(1)}, f32[256,256]{1,0:T(8,128)}, u32[]{:S(2)}) copy-start(f32[256,256]{1,0:T(8,128)} %param.14) | copy-start | bytes 786436
  7.2 24.6 %copy-start.26 = (bf16[256,256]{1,0:T(8,128)(2,1)S(1)}, bf16[256,256]{1,0:T(8,128)(2,1)}, u32[]{:S(2)}) copy-start(bf16[256,256]{1,0:T(8,128)(2,1)} %param.17) | copy-start | bytes 393220
  7.2 218.1 %all-gather.2.cloned.1.call-start = ((), (), s32[]{:S(2)}) async-start(), calls=%async_computation.4 | async-start | bytes 2621440 | tf_op jit(solution)/shard_map/all_gather | solution.py:216
  26.3 6.8 %copy-start.48 = (f32[256]{0:T(256)S(1)}, f32[256]{0:T(256)}, u32[]{:S(2)}) copy-start(f32[256]{0:T(256)} %param.16) | copy-start | bytes 3076
  26.3 7.4 %copy-start.50 = (f32[256]{0:T(256)S(1)}, f32[256]{0:T(256)}, u32[]{:S(2)}) copy-start(f32[256]{0:T(256)} %param.23) | copy-start | bytes 3076
  26.3 396.3 %reduce-scatter.3.cloned.1.call-start = ((), (), s32[]{:S(2)}) async-start(), calls=%async_computation.2 | async-start | bytes 2621440 | tf_op jit(solution)/shard_map/reduce_scatter | solution.py:299
  30.0 39.2 %copy-start.14 = (bf16[256,1152]{1,0:T(8,128)(2,1)S(1)}, bf16[256,1152]{1,0:T(8,128)(2,1)}, u32[]{:S(2)}) copy-start(bf16[256,1152]{1,0:T(8,128)(2,1)} %param.24) | copy-start | bytes 1769476
  31.9 37.7 %copy-start.15 = (bf16[256,1152]{1,0:T(8,128)(2,1)S(1)}, bf16[256,1152]{1,0:T(8,128)(2,1)}, u32[]{:S(2)}) copy-start(bf16[256,1152]{1,0:T(8,128)(2,1)} %param.25) | copy-start | bytes 1769476
  66.3 3.6 copy-start.25
  71.2 34.9 %copy-start.12 = (bf16[1024,192]{1,0:T(8,128)(2,1)S(1)}, bf16[1024,192]{1,0:T(8,128)(2,1)}, u32[]{:S(2)}) copy-start(bf16[1024,192]{1,0:T(8,128)(2,1)} %get-tuple-element.39) | copy-start | bytes 1179652
  106.0 3.8 copy-start.55
  106.0 3.8 copy-start.57
  106.1 4.5 copy-start.37
  111.6 1.9 copy-start.5
  113.6 36.7 %copy-start.21 = (bf16[1024,64]{0,1:T(8,128)(2,1)}, bf16[1024,64]{0,1:T(8,128)(2,1)S(1)}, u32[]{:S(2)}) copy-start(bf16[1024,64]{0,1:T(8,128)(2,1)S(1)} %fusion.23) | copy-start | bytes 393220
  153.2 37.6 %copy-start.47 = (f32[1,1024]{1,0:T(1,128)S(1)}, f32[1,1024]{1,0:T(1,128)}, u32[]{:S(2)}) copy-start(f32[1,1024]{1,0:T(1,128)} %slice.170) | copy-start | bytes 12292
  190.8 2.0 copy-start.40
  219.7 3.8 copy-start
  219.7 3.8 copy-start.2
  229.8 4.9 copy-start.19
  240.8 4.1 copy-start.4
  244.8 247.7 %all-reduce.4.cloned.1.call-start = ((), (), s32[]{:S(2)}) async-start(), calls=%async_computation.5 | async-start | bytes 4325376 | tf_op jit(solution)/shard_map/psum | solution.py:398
  293.8 19.4 %copy-start.8 = (f32[256,256]{1,0:T(8,128)S(1)}, f32[256,256]{1,0:T(8,128)}, u32[]{:S(2)}) copy-start(f32[256,256]{1,0:T(8,128)} %param.27) | copy-start | bytes 786436
  293.8 19.4 %copy-start.41 = (f32[1,256]{1,0:T(1,128)S(1)}, f32[1,256]{1,0:T(1,128)}, u32[]{:S(2)}) copy-start(f32[1,256]{1,0:T(1,128)} %copy-done.40) | copy-start | bytes 3076
  293.8 19.4 %copy-start.51 = (f32[256]{0:T(256)S(1)}, f32[256]{0:T(256)}, u32[]{:S(2)}) copy-start(f32[256]{0:T(256)} %param.23) | copy-start | bytes 3076
  293.8 40.6 %copy-start.16 = (bf16[4,256,288]{2,1,0:T(8,128)(2,1)S(1)}, bf16[4,256,288]{2,1,0:T(8,128)(2,1)}, u32[]{:S(2)}) copy-start(bf16[4,256,288]{2,1,0:T(8,128)(2,1)} %get-tuple-element.55) | copy-start | bytes 1769476
  310.9 24.6 %copy-start.10 = (bf16[256,1024]{1,0:T(8,128)(2,1)S(1)}, bf16[256,1024]{1,0:T(8,128)(2,1)}, u32[]{:S(2)}) copy-start(bf16[256,1024]{1,0:T(8,128)(2,1)} %get-tuple-element.42) | copy-start | bytes 1572868
  334.3 6.6 %copy-start.53 = (f32[256]{0:T(256)}, f32[256]{0:T(256)S(1)}, u32[]{:S(2)}) copy-start(f32[256]{0:T(256)S(1)} %fusion.87) | copy-start | bytes 3076
  340.9 29.4 %copy-start.44 = (f32[1024]{0:T(1024)S(1)}, f32[1024]{0:T(1024)}, u32[]{:S(2)}) copy-start(f32[1024]{0:T(1024)} %copy-done.43) | copy-start | bytes 12292
  370.3 3.8 copy-start.6
  374.2 2.4 copy-start.32
  374.2 2.4 copy-start.34
  379.4 2.0 copy-start.23
  379.4 2.6 copy-start.11
  382.1 3.4 copy-start.1
  382.1 3.4 copy-start.22
  383.4 3.2 copy-start.24
  419.1 4.1 copy-start.9
  422.5 90.0 %reduce-scatter.5.cloned.1.call-start = ((), (), s32[]{:S(2)}) async-start(), calls=%async_computation.3 | async-start | bytes 655360 | tf_op jit(solution)/shard_map/reduce_scatter | solution.py:298
  422.6 16.4 %copy-start.59 = (f32[256]{0:T(256)S(1)}, f32[256]{0:T(256)}, u32[]{:S(2)}) copy-start(f32[256]{0:T(256)} %get-tuple-element.104) | copy-start | bytes 3076
  423.1 17.3 %copy-start.39 = (f32[1,256]{1,0:T(1,128)S(1)}, f32[1,256]{1,0:T(1,128)}, u32[]{:S(2)}) copy-start(f32[1,256]{1,0:T(1,128)} %copy-done.38) | copy-start | bytes 3076
  423.2 17.3 %copy-start.49 = (f32[256]{0:T(256)S(1)}, f32[256]{0:T(256)}, u32[]{:S(2)}) copy-start(f32[256]{0:T(256)} %param.16) | copy-start | bytes 3076
  423.2 17.7 %copy-start.60 = (f32[64]{0:T(128)S(1)}, f32[64]{0:T(128)}, u32[]{:S(2)}) copy-start(f32[64]{0:T(128)} %get-tuple-element.101) | copy-start | bytes 772
  492.5 9.0 %copy-start.18 = (bf16[256,1152]{0,1:T(8,128)(2,1)S(1)}, bf16[256,1152]{0,1:T(8,128)(2,1)}, u32[]{:S(2)}) copy-start(bf16[256,1152]{0,1:T(8,128)(2,1)} %get-tuple-element.118) | copy-start | bytes 1769476
  495.9 6.9 %copy-start.17 = (bf16[1152,256]{1,0:T(8,128)(2,1)S(1)}, bf16[1152,256]{1,0:T(8,128)(2,1)}, u32[]{:S(2)}) copy-start(bf16[1152,256]{1,0:T(8,128)(2,1)} %get-tuple-element.120) | copy-start | bytes 1769476
  501.5 11.0 %copy-start.42 = (f32[1,256]{1,0:T(1,128)S(1)}, f32[1,256]{1,0:T(1,128)}, u32[]{:S(2)}) copy-start(f32[1,256]{1,0:T(1,128)} %copy-done.40) | copy-start | bytes 3076
  501.5 11.0 %copy-start.52 = (f32[256]{0:T(256)S(1)}, f32[256]{0:T(256)}, u32[]{:S(2)}) copy-start(f32[256]{0:T(256)} %param.23) | copy-start | bytes 3076
  501.5 11.0 %copy-start.54 = (f32[256]{0:T(256)S(1)}, f32[256]{0:T(256)}, u32[]{:S(2)}) copy-start(f32[256]{0:T(256)} %copy-done.53) | copy-start | bytes 3076
  (19 other events, 25.0 us)
Sparse Core Ops, SparseCore 0:
  26.4 24.4 all-gather.1
  244.9 43.1 reduce-scatter.2
  422.7 65.8 all-reduce.3
  490.7 21.8 reduce-scatter.4

commit v2 on v1

--- a/solution.py
+++ b/solution.py
@@ -69,14 +69,230 @@
     return ref.at[(slice(None),) * dim + (pl.ds(start, size),)]
 
 
-def swap_kernel(ops, sizes, *refs):
-    count = len(ops)
-    ins, outs = refs[:count], refs[count : 2 * count]
-    send_sem, recv_sem, own_sem = refs[2 * count :]
-    axes = sorted({op[0] for op in ops})
-    me = {axis: lax.axis_index(axis) for axis in axes}
+def send_to(src, dst, sends, recvs, slot, axis, peer):
+    copy = pltpu.make_async_remote_copy(
+        src_ref=src,
+        dst_ref=dst,
+        send_sem=sends.at[slot],
+        recv_sem=recvs.at[slot],
+        device_id={axis: peer},
+        device_id_type=pl.DeviceIdType.MESH,
+    )
+    copy.start()
+    return copy
+
+
+def push_steps(plan, n, me, ins, outs, scratch):
+    axis, src_dim, src_size, dst_dim, dst_size = plan
+    sends, recvs, own = scratch
+    copies = []
+    for step in range(1, n):
+        peer = lax.rem(me + step, n)
+        copies.append(
+            send_to(
+                part(ins[0], src_dim, peer, src_size),
+                part(outs[0], dst_dim, me, dst_size),
+                sends,
+                recvs,
+                step - 1,
+                axis,
+                peer,
+            )
+        )
+    copy = pltpu.make_async_copy(
+        part(ins[0], src_dim, me, src_size), part(outs[0], dst_dim, me, dst_size), own.at[0]
+    )
+    copy.start()
+    copies.append(copy)
+    yield
+    yield
+    yield
+    for copy in copies:
+        copy.wait()
+
+
+def partners(me):
+    near = me + 1 - 2 * lax.rem(me, 2)
+    far = lax.rem(me + 2, 4)
+    return near, far, lax.rem(near + 2, 4)
+
+
+def span(block, rows, piece, pieces):
+    size = rows // pieces
+    return pl.ds(pl.multiple_of(block * rows + piece * size, size), size)
+
+
+def relay_gather_steps(plan, n, me, ins, outs, scratch):
+    axis, pieces = plan
+    sends, recvs, own = scratch
+    rows = ins[0].shape[0]
+    near, far, _ = partners(me)
+    size = rows // pieces
+    firsts = [
+        send_to(
+            ins[0].at[pl.ds(p * size, size)],
+            outs[0].at[span(me, rows, p, pieces)],
+            sends,
+            recvs,
+            p,
+            axis,
+            far,
+        )
+        for p in range(pieces)
+    ]
+    beside = send_to(
+        ins[0], outs[0].at[span(me, rows, 0, 1)], sends, recvs, pieces, axis, near
+    )
+    mine = pltpu.make_async_copy(ins[0], outs[0].at[span(me, rows, 0, 1)], own.at[0])
+    mine.start()
+    yield
+    relays = []
+    for p in range(pieces):
+        firsts[p].wait_recv()
+        place = span(far, rows, p, pieces)
+        relays.append(
+            send_to(
+                outs[0].at[place], outs[0].at[place], sends, recvs, pieces + 1 + p, axis, near
+            )
+        )
+    yield
+    for copy in firsts:
+        copy.wait_send()
+    beside.wait()
+    for copy in relays:
+        copy.wait()
+    mine.wait()
+
+
+def relay_reduce_steps(plan, n, me, ins, outs, scratch):
+    axis, pieces = plan
+    sends, recvs, from_near, passed, from_far = scratch
+    flt = jnp.float32
+    rows = outs[0].shape[0]
+    size = rows // pieces
+    near, far, across = partners(me)
+    firsts = [
+        send_to(
+            ins[0].at[span(across, rows, p, pieces)],
+            from_near.at[pl.ds(p * size, size)],
+            sends,
+            recvs,
+            p,
+            axis,
+            near,
+        )
+        for p in range(pieces)
+    ]
+    beside = send_to(
+        ins[0].at[span(near, rows, 0, 1)],
+        from_near.at[pl.ds(rows, rows)],
+        sends,
+        recvs,
+        pieces,
+        axis,
+        near,
+    )
+    yield
+    seconds = []
+    for p in range(pieces):
+        here = pl.ds(p * size, size)
+        firsts[p].wait_recv()
+        passed[here, :] = (
+            ins[0][span(far, rows, p, pieces), :].astype(flt) + from_near[here, :].astype(flt)
+        ).astype(passed.dtype)
+        seconds.append(
+            send_to(
+                passed.at[here], from_far.at[here], sends, recvs, pieces + 1 + p, axis, far
+            )
+        )
+    beside.wait_recv()
+    yield
+    for p in range(pieces):
+        here = pl.ds(p * size, size)
+        seconds[p].wait_recv()
+        outs[0][here, :] = (
+            ins[0][span(me, rows, p, pieces), :].astype(flt)
+            + from_near[pl.ds(rows + p * size, size), :].astype(flt)
+            + from_far[here, :].astype(flt)
+        ).astype(outs[0].dtype)
+    for copy in firsts + [beside] + seconds:
+        copy.wait_send()
+
+
+def reduce_gather_steps(plan, n, me, ins, outs, scratch):
+    axis, pieces, added_to, gained = plan
+    sends, recvs, got, mine = scratch
+    flt = jnp.float32
+    rows, width = outs[0].shape
+    size = rows // pieces
+    own_columns = pl.ds(pl.multiple_of(me * width, width), width)
+    arriving = []
+    for p in range(pieces):
+        here = pl.ds(p * size, size)
+        arriving.append(
+            [
+                send_to(
+                    ins[0].at[
+                        here,
+                        pl.ds(pl.multiple_of(lax.rem(me + step, n) * width, width), width),
+                    ],
+                    got.at[step - 1, here],
+                    sends,
+                    recvs,
+                    p * (n - 1) + step - 1,
+                    axis,
+                    lax.rem(me + step, n),
+                )
+                for step in range(1, n)
+            ]
+        )
+    yield
+    leaving = []
+    for p in range(pieces):
+        here = pl.ds(p * size, size)
+        total = ins[0][here, own_columns].astype(flt)
+        for step in range(1, n):
+            arriving[p][step - 1].wait_recv()
+            total = total + got[step - 1, here].astype(flt)
+        if added_to:
+            total = total + ins[1][here, :]
+        outs[0][here, :] = total
+        if gained:
+            total = total * ins[1][0:1, :]
+        mine[here, :] = total.astype(mine.dtype)
+        outs[1][here, own_columns] = total.astype(mine.dtype)
+        for step in range(1, n):
+            leaving.append(
+                send_to(
+                    mine.at[here],
+                    outs[1].at[here, own_columns],
+                    sends,
+                    recvs,
+                    (pieces + p) * (n - 1) + step - 1,
+                    axis,
+                    lax.rem(me + step, n),
+                )
+            )
+    yield
+    for copies in arriving:
+        for copy in copies:
+            copy.wait_send()
+    for copy in leaving:
+        copy.wait()
+
+
+STEPS = {
+    "push": push_steps,
+    "relay_gather": relay_gather_steps,
+    "relay_reduce": relay_reduce_steps,
+    "reduce_gather": reduce_gather_steps,
+}
+
+
+def exchange_kernel(jobs, sizes, *refs):
+    me = {axis: lax.axis_index(axis) for axis in sizes}
     barrier = pltpu.get_barrier_semaphore()
-    for axis in axes:
+    for axis in sizes:
         for step in range(1, sizes[axis]):
             pl.semaphore_signal(
                 barrier,
@@ -84,67 +300,116 @@
                 device_id={axis: lax.rem(me[axis] + step, sizes[axis])},
                 device_id_type=pl.DeviceIdType.MESH,
             )
-    pl.semaphore_wait(barrier, sum(sizes[axis] - 1 for axis in axes))
-    copies = []
-    slot = 0
-    for place, (axis, src_dim, src_size, dst_dim, dst_size) in enumerate(ops):
-        for step in range(1, sizes[axis]):
-            peer = lax.rem(me[axis] + step, sizes[axis])
-            copy = pltpu.make_async_remote_copy(
-                src_ref=part(ins[place], src_dim, peer, src_size),
-                dst_ref=part(outs[place], dst_dim, me[axis], dst_size),
-                send_sem=send_sem.at[slot],
-                recv_sem=recv_sem.at[slot],
-                device_id={axis: peer},
-                device_id_type=pl.DeviceIdType.MESH,
-            )
-            copy.start()
-            copies.append(copy)
-            slot += 1
-    for place, (axis, src_dim, src_size, dst_dim, dst_size) in enumerate(ops):
-        copy = pltpu.make_async_copy(
-            part(ins[place], src_dim, me[axis], src_size),
-            part(outs[place], dst_dim, me[axis], dst_size),
-            own_sem.at[place],
-        )
-        copy.start()
-        copies.append(copy)
-    for copy in copies:
-        copy.wait()
-
-
-def swap(ident, *ops):
-    sizes = {op[0]: lax.axis_size(op[0]) for op in ops}
-    plans, shapes = [], []
-    for axis, array, src_dim, dst_dim in ops:
-        n = sizes[axis]
-        block = list(array.shape)
-        src_size = dst_size = None
-        if src_dim == "lead":
-            block = block[1:]
-        elif src_dim is not None:
-            block[src_dim] //= n
-            src_size = block[src_dim]
-        if dst_dim == "lead":
-            block = [n] + block
-        else:
-            dst_size = block[dst_dim]
-            block[dst_dim] *= n
-        plans.append((axis, src_dim, src_size, dst_dim, dst_size))
-        shapes.append(jax.ShapeDtypeStruct(tuple(block), array.dtype))
-    slots = sum(sizes[op[0]] - 1 for op in ops)
+    pl.semaphore_wait(barrier, sum(sizes[axis] - 1 for axis in sizes))
+    refs = list(refs)
+    taken = []
+    for field in (2, 3, 4):
+        taken.append([])
+        for job in jobs:
+            taken[-1].append([refs.pop(0) for _ in range(job[field])])
+    running = [
+        STEPS[job[0]](job[1], sizes[job[1][0]], me[job[1][0]], *[group[i] for group in taken])
+        for i, job in enumerate(jobs)
+    ]
+    while running:
+        running = [steps for steps in running if next(steps, "over") != "over"]
+
+
+def push(axis, array, src_dim, dst_dim):
+    n = lax.axis_size(axis)
+    block = list(array.shape)
+    src_size = dst_size = None
+    if src_dim == "lead":
+        block = block[1:]
+    elif src_dim is not None:
+        block[src_dim] //= n
+        src_size = block[src_dim]
+    if dst_dim == "lead":
+        block = [n] + block
+    else:
+        dst_size = block[dst_dim]
+        block[dst_dim] *= n
+    sems = pltpu.SemaphoreType.DMA((n - 1,))
+    return (
+        "push",
+        (axis, src_dim, src_size, dst_dim, dst_size),
+        [array],
+        [jax.ShapeDtypeStruct(tuple(block), array.dtype)],
+        [sems, sems, pltpu.SemaphoreType.DMA((1,))],
+    )
+
+
+def gather_rows(axis, array, pieces=2):
+    if lax.axis_size(axis) != 4:
+        return push(axis, array, None, 0)
+    sems = pltpu.SemaphoreType.DMA((2 * pieces + 1,))
+    return (
+        "relay_gather",
+        (axis, pieces),
+        [array],
+        [jax.ShapeDtypeStruct((4 * array.shape[0],) + array.shape[1:], array.dtype)],
+        [sems, sems, pltpu.SemaphoreType.DMA((1,))],
+    )
+
+
+def reduce_rows(axis, array, pieces=2):
+    if lax.axis_size(axis) != 4:
+        return push(axis, array, 0, "lead")
+    rows, width = array.shape[0] // 4, array.shape[1]
+    sems = pltpu.SemaphoreType.DMA((2 * pieces + 1,))
+    return (
+        "relay_reduce",
+        (axis, pieces),
+        [array],
+        [jax.ShapeDtypeStruct((rows, width), array.dtype)],
+        [
+            sems,
+            sems,
+            pltpu.VMEM((2 * rows, width), array.dtype),
+            pltpu.VMEM((rows, width), array.dtype),
+            pltpu.VMEM((rows, width), array.dtype),
+        ],
+    )
+
+
+def reduce_then_gather(axis, array, base=None, gain=None, pieces=2):
+    n = lax.axis_size(axis)
+    rows, width = array.shape[0], array.shape[1] // n
+    sems = pltpu.SemaphoreType.DMA((2 * pieces * (n - 1),))
+    return (
+        "reduce_gather",
+        (axis, pieces, base is not None, gain is not None),
+        [array] + [x for x in (base, gain) if x is not None],
+        [
+            jax.ShapeDtypeStruct((rows, width), jnp.float32),
+            jax.ShapeDtypeStruct(array.shape, array.dtype),
+        ],
+        [
+            sems,
+            sems,
+            pltpu.VMEM((n - 1, rows, width), array.dtype),
+            pltpu.VMEM((rows, width), array.dtype),
+        ],
+    )
+
+
+def exchange(ident, *jobs):
+    sizes = {job[1][0]: lax.axis_size(job[1][0]) for job in jobs}
+    ins = [array for job in jobs for array in job[2]]
+    outs = [shape for job in jobs for shape in job[3]]
+    whole = pl.BlockSpec(memory_space=pltpu.VMEM)
     return pl.pallas_call(
-        functools.partial(swap_kernel, tuple(plans), sizes),
-        out_shape=tuple(shapes),
-        in_specs=[pl.BlockSpec(memory_space=pltpu.VMEM)] * len(ops),
-        out_specs=(pl.BlockSpec(memory_space=pltpu.VMEM),) * len(ops),
-        scratch_shapes=[
-            pltpu.SemaphoreType.DMA((slots,)),
-            pltpu.SemaphoreType.DMA((slots,)),
-            pltpu.SemaphoreType.DMA((len(ops),)),
-        ],
+        functools.partial(
+            exchange_kernel,
+            tuple((job[0], job[1], len(job[2]), len(job[3]), len(job[4])) for job in jobs),
+            sizes,
+        ),
+        out_shape=tuple(outs),
+        in_specs=[whole] * len(ins),
+        out_specs=(whole,) * len(outs),
+        scratch_shapes=[scratch for job in jobs for scratch in job[4]],
         compiler_params=pltpu.CompilerParams(collective_id=ident, has_side_effects=True),
-    )(*[op[1] for op in ops])
+    )(*ins)
 
 
 def dot(left_side, right_side):
@@ -169,6 +434,26 @@
 
 def added(stacked):
     return jnp.sum(stacked.astype(jnp.float32), axis=0)
+
+
+def joined(reduced):
+    return reduced if reduced.ndim == 2 else added(reduced).astype(reduced.dtype)
+
+
+def row_rates(wide):
+    return lax.rsqrt(jnp.mean(wide * wide, axis=1, keepdims=True) + epsilon)
+
+
+def unfold(got):
+    return jnp.moveaxis(got, 0, 1).reshape(got.shape[1], -1)
+
+
+def dp_jobs(array):
+    return [push("dp", array, None, "lead")] if lax.axis_size("dp") == 2 else []
+
+
+def dp_total(array, got):
+    return added(got[0]) if got else lax.psum(array, "dp").astype(jnp.float32)
 
 
 def local(
@@ -213,10 +498,6 @@
     cos_table, sin_table = rotary_tables(positions_of(documents))
 
     cot_low = cotangent.astype(low)
-    cot_all = lax.all_gather(
-        lax.all_gather(cot_low, "row", axis=1, tiled=True), "col", axis=0, tiled=True
-    )
-
     w_joined_parts = jnp.stack(
         [
             jnp.concatenate(
@@ -236,20 +517,20 @@
             for r in range(rows)
         ]
     )
-    hidden_row, square_in, norm_in_all, norm_mid_all, w_joined, w_out_mine = swap(
+    hidden_row, norm_in_all, norm_mid_all, w_joined, w_out_mine = exchange(
         0,
-        ("row", hidden_in.astype(low), None, 1),
-        ("row", eight(jnp.sum(hidden_in * hidden_in, axis=1)), None, "lead"),
-        ("row", eight(norm_in), None, 1),
-        ("row", eight(norm_mid), None, 1),
-        ("row", w_joined_parts, "lead", 0),
-        ("row", w_out, 0, 1),
-    )
-    rate_in = lax.rsqrt(jnp.sum(square_in, axis=0)[0] / model_width + epsilon)[:, None]
-    normed_in, w_pair = swap(
+        push("row", hidden_in.astype(low), None, 1),
+        push("row", eight(norm_in), None, 1),
+        push("row", eight(norm_mid), None, 1),
+        push("row", w_joined_parts, "lead", 0),
+        push("row", w_out, 0, 1),
+    )
+    hidden_wide = hidden_row.astype(flt)
+    rate_in = row_rates(hidden_wide)
+    normed_in, w_pair = exchange(
         1,
-        ("col", (hidden_row.astype(flt) * rate_in * norm_in_all[:1]).astype(low), None, 0),
-        ("row", w_pair_parts, "lead", 1),
+        gather_rows("col", (hidden_wide * rate_in * norm_in_all[:1]).astype(low)),
+        push("row", w_pair_parts, "lead", 1),
     )
     projected = dot(normed_in, w_joined)
     raw_query = projected[:, :q_width].reshape(stream, q_mine, HEAD_DIM)
@@ -273,21 +554,19 @@
         .reshape(stream, q_width)
         .astype(low)
     )
-    out_parts, w_down_mine = swap(
+    out_cols, cot_row = exchange(
         2,
-        ("col", dot(mixed, w_out_mine).astype(low), 0, "lead"),
-        ("row", w_down, 0, 1),
-    )
-    (out_cols,) = swap(3, ("row", added(out_parts).astype(low), 1, "lead"))
-    resid = hidden_in + added(out_cols)
-    resid_row, square_mid = swap(
+        reduce_rows("col", dot(mixed, w_out_mine).astype(low)),
+        push("row", cot_low, None, 1),
+    )
+    cot_all = lax.all_gather(cot_row, "col", axis=0, tiled=True)
+    resid, resid_row = exchange(3, reduce_then_gather("row", joined(out_cols), base=hidden_in))
+    resid_wide = resid_row.astype(flt)
+    rate_mid = row_rates(resid_wide)
+    normed_mid, w_down_mine = exchange(
         4,
-        ("row", resid.astype(low), None, 1),
-        ("row", eight(jnp.sum(resid * resid, axis=1)), None, "lead"),
-    )
-    rate_mid = lax.rsqrt(jnp.sum(square_mid, axis=0)[0] / model_width + epsilon)[:, None]
-    (normed_mid,) = swap(
-        5, ("col", (resid_row.astype(flt) * rate_mid * norm_mid_all[:1]).astype(low), None, 0)
+        gather_rows("col", (resid_wide * rate_mid * norm_mid_all[:1]).astype(low)),
+        push("row", w_down, 0, 1),
     )
     gate_pre = dot(normed_mid, w_pair[0])
     up_pre = dot(normed_mid, w_pair[1])
@@ -311,37 +590,34 @@
     mid_part = dot_turned(grad_gate_act, w_pair[0]) + dot_turned(grad_up_act, w_pair[1])
     grad_gate = outer_sum(normed_mid, grad_gate_act).astype(low)
     grad_up = outer_sum(normed_mid, grad_up_act).astype(low)
-    mid_parts, grad_gate_got, grad_up_got = swap(
+    mid_cols, grad_down, *pair = exchange(
+        5,
+        reduce_rows("col", mid_part.astype(low)),
+        push("row", grad_down, 1, 0),
+        *dp_jobs(grad_gate),
+    )
+    grad_gate = dp_total(grad_gate, pair).astype(low)
+    grad_normed_mid, scaled_row, *pair = exchange(
         6,
-        ("col", mid_part.astype(low), 0, "lead"),
-        ("row", grad_gate, 0, "lead"),
-        ("row", grad_up, 0, "lead"),
-    )
-    (mid_cols,) = swap(7, ("row", added(mid_parts).astype(low), 1, "lead"))
-    grad_normed_mid = added(mid_cols)
-    scaled_mid = norm_mid * grad_normed_mid
-    first_mid = cotangent + rate_mid * scaled_mid
-    first_row, inner_got = swap(
-        8,
-        ("row", first_mid.astype(low), None, 1),
-        ("row", eight(jnp.sum(scaled_mid * resid, axis=1)), None, "lead"),
-    )
-    mid_scale = rate_mid**3 * (jnp.sum(inner_got, axis=0)[0][:, None] / model_width)
-    grad_resid = first_mid - resid * mid_scale
+        reduce_then_gather("row", joined(mid_cols), gain=eight(norm_mid)),
+        *dp_jobs(grad_up),
+        *dp_jobs(grad_down),
+    )
+    grad_up = dp_total(grad_up, pair[:1]).astype(low)
+    grad_down = dp_total(grad_down, pair[1:])
+    scaled_wide = scaled_row.astype(flt)
+    mid_scale = rate_mid**3 * jnp.mean(scaled_wide * resid_wide, axis=1, keepdims=True)
+    grad_resid = cotangent + rate_mid * (norm_mid * grad_normed_mid) - resid * mid_scale
     gain_mid = jnp.sum(grad_normed_mid * resid * rate_mid, axis=0)
-    resid_low, grad_down_got = swap(
-        9,
-        ("col", (first_row.astype(flt) - resid_row.astype(flt) * mid_scale).astype(low), None, 0),
-        ("row", grad_down, 1, 0),
-    )
-
-    def unfold(got):
-        return jnp.moveaxis(got, 0, 1).reshape(got.shape[1], -1)
-
-    grad_gate, grad_up, grad_down = (
-        value.astype(flt)
-        for value in lax.psum((unfold(grad_gate_got), unfold(grad_up_got), grad_down_got), "dp")
-    )
+    resid_low, grad_gate_got = exchange(
+        7,
+        gather_rows(
+            "col",
+            (cot_row.astype(flt) + rate_mid * scaled_wide - resid_wide * mid_scale).astype(low),
+        ),
+        push("row", grad_gate, 0, "lead"),
+    )
+    grad_gate = unfold(grad_gate_got).astype(flt)
     grad_out = outer_sum(mixed, resid_low).astype(low)
     grad_mixed_heads = (
         dot_turned(resid_low, w_out_mine).astype(low).reshape(stream, kv_mine, groups, HEAD_DIM)
@@ -375,44 +651,50 @@
         axis=1,
     ).astype(low)
     grad_joined = outer_sum(normed_in, grad_proj).astype(low)
-    in_parts, joined_got, out_got = swap(
-        10,
-        ("col", dot_turned(grad_proj, w_joined).astype(low), 0, "lead"),
-        ("row", grad_joined, 0, "lead"),
-        ("row", grad_out, 1, 0),
-    )
-    (in_cols,) = swap(11, ("row", added(in_parts).astype(low), 1, "lead"))
-    grad_normed_in = added(in_cols)
-    scaled_in = norm_in * grad_normed_in
-    (in_inner,) = swap(12, ("row", eight(jnp.sum(scaled_in * hidden_in, axis=1)), None, "lead"))
+    in_part = dot_turned(grad_proj, w_joined)
+    block_start = lax.axis_index("row") * feature_slab
+    gain_in = jnp.sum(in_part * normed_in.astype(flt), axis=0) / norm_in_all[0]
+    spread_mid = lax.dynamic_update_slice(jnp.zeros((model_width,), flt), gain_mid, (block_start,))
+    gains = jnp.concatenate([gain_in, spread_mid, gain_query, gain_key])
+    in_cols, grad_up_got, gains_got, *pair = exchange(
+        8,
+        reduce_rows("col", in_part.astype(low)),
+        push("row", grad_up, 0, "lead"),
+        push("dp", eight(gains), None, "lead"),
+        *dp_jobs(grad_joined),
+        *dp_jobs(grad_out),
+    )
+    in_cols = joined(in_cols)
+    inner_part = jnp.sum(in_cols.astype(flt) * hidden_wide * norm_in_all[:1], axis=1)
+    grad_up = unfold(grad_up_got).astype(flt)
+    grad_joined = dp_total(grad_joined, pair[:1]).astype(low)
+    grad_out = dp_total(grad_out, pair[1:]).astype(low)
+    in_blocks, in_inner, joined_got, out_got, gains_got = exchange(
+        9,
+        push("row", in_cols, 1, "lead"),
+        push("row", eight(inner_part), None, "lead"),
+        push("row", grad_joined, 0, "lead"),
+        push("row", grad_out, 1, 0),
+        push("row", jnp.sum(gains_got, axis=0), None, "lead"),
+    )
+    (gains_got,) = exchange(10, push("col", jnp.sum(gains_got, axis=0), None, "lead"))
+    gains = jnp.sum(gains_got, axis=0)[0]
+    grad_normed_in = added(in_blocks)
     in_scale = rate_in**3 * (jnp.sum(in_inner, axis=0)[0][:, None] / model_width)
-    grad_hidden = grad_resid + rate_in * scaled_in - hidden_in * in_scale
-    gain_in = jnp.sum(grad_normed_in * hidden_in * rate_in, axis=0)
+    grad_hidden = grad_resid + rate_in * (norm_in * grad_normed_in) - hidden_in * in_scale
 
     def shared(got):
         summed = got.astype(flt).reshape(rows // share, share, feature_slab, k_width).sum(axis=1)
-        return unfold(summed).astype(low)
-
-    grad_query, grad_key, grad_value, grad_out = (
-        value.astype(flt)
-        for value in lax.psum(
-            (
-                unfold(joined_got[:, :, :q_width]),
-                shared(joined_got[:, :, q_width : q_width + k_width]),
-                shared(joined_got[:, :, q_width + k_width :]),
-                out_got,
-            ),
-            "dp",
-        )
-    )
-    block_start = lax.axis_index("row") * feature_slab
-    spread_in = lax.dynamic_update_slice(jnp.zeros((model_width,), flt), gain_in, (block_start,))
-    spread_mid = lax.dynamic_update_slice(jnp.zeros((model_width,), flt), gain_mid, (block_start,))
-    sum_in, sum_mid, gain_query, gain_key = lax.psum(
-        (spread_in, spread_mid, gain_query, gain_key), ("dp", "row", "col")
-    )
-    gain_in = lax.dynamic_slice(sum_in, (block_start,), (feature_slab,))
-    gain_mid = lax.dynamic_slice(sum_mid, (block_start,), (feature_slab,))
+        return unfold(summed)
+
+    grad_query = unfold(joined_got[:, :, :q_width]).astype(flt)
+    grad_key = shared(joined_got[:, :, q_width : q_width + k_width])
+    grad_value = shared(joined_got[:, :, q_width + k_width :])
+    grad_out = out_got.astype(flt)
+    gain_in = lax.dynamic_slice(gains, (block_start,), (feature_slab,))
+    gain_mid = lax.dynamic_slice(gains, (model_width + block_start,), (feature_slab,))
+    gain_query = gains[2 * model_width : 2 * model_width + HEAD_DIM]
+    gain_key = gains[2 * model_width + HEAD_DIM :]
     return (
         output,
         grad_hidden,

time: 523 us -> 450 us (0.86)
  blocking collectives: 60.1 us -> 0 us
  Pallas kernels: 314 us -> 295 us
  waiting for transfers between devices: 9.19 us -> 19.2 us
  local copies, waits for them, and re-layouts: 34.7 us -> 27.1 us
    psum x1 -> x0, blocking collectives: 42.1 us -> none  [local(): lax.psum((spread_in, spread_mid, gain_query, gain_key), ('dp', 'row', 'co...]
    pallas_call x13 -> x11, Pallas kernels: 314 us -> 295 us  [exchange(): pl.pallas_call(functools.partial(exchange_kernel, tuple(((job[0], job[1],...]
    all_gather x1 -> x0, blocking collectives: 18 us -> none  [local(): lax.all_gather(cot_low, 'row', axis=1, tiled=True)]
    reduce_scatter x1, waiting for transfers between devices: 8.62 us -> 19.2 us  [local(): lax.psum_scatter(lax.psum_scatter(down_part, 'col', scatter_dimension=0,...]
    unnamed x131 -> x147, local copies, waits for them, and re-layouts: 10.7 us -> 8.48 us
  transfers between devices with their start and end apart: 4 -> 3, of which waited for: 1 -> 1; matrix products, arithmetic and copies ran while one was open for 19% -> 16% of each run, Pallas kernels for 60% -> 45%
where the time goes in v2:
time: 450 us; the launch traced here: 448 us
  Pallas kernels  295 us (66%)
  matrix products  47.7 us (11%)
  other arithmetic  43.5 us (10%)
  local copies, waits for them, and re-layouts  27.1 us (6%)
  waiting for transfers between devices  19.2 us (4%)
  between operations  15.5 us (3%)
    pallas_call x11, Pallas kernels, exchange(): pl.pallas_call(functools.partial(exchange_kernel, tuple(((job[0], job[1],...  295 us
    reduce_scatter x1, waiting for transfers between devices, local(): lax.psum_scatter(lax.psum_scatter(down_part, 'col', scatter_dimension=0,...  19.2 us
    dot_general x5, matrix products, dot_turned(): lax.dot_general(left_side, right_side, (((1,), (1,)), ((), ())), preferre...  17.3 us
    dot_general x5, matrix products, dot(): return jnp.dot(left_side, right_side, preferred_element_type=jnp.float32)  14.2 us
    reduce_sum x6, other arithmetic, added(): return jnp.sum(stacked.astype(jnp.float32), axis=0)  12.2 us
  transfers between devices with their start and end apart: 3, of which 1 were waited for; matrix products, arithmetic and copies ran while one was open for 16% of the time, Pallas kernels for 45%

profile of v2, /device:TPU:0, one launch (start us, length us, event | category | flops | bytes accessed | tf_op | source)
XLA Modules:
  0.0 448.4 jit_solution(10637318083583628754)
XLA Ops:
  10.0 1.6 convert_element_type.170.refs_1_
  11.6 1.6 convert_element_type.160.refs_0_
  18.6 34.5 %shard_map.240 = (bf16[256,1024]{1,0:T(8,128)(2,1)}, f32[8,1024]{1,0:T(8,128)}, f32[8,1024]{1,0:T(8,128)}, bf16[1024,192]{1,0:T(8,128)(2,1)}, bf16[64,1024]{1,0:T(8,128)(2,1)}) custom-call(bf16[256,256]{1,0:T(8,128)(2,1)} %convert_element_type.160.refs_0_, f32[8,256]{1,0:T(8,128)} %broadcast_in_dim.20.refs_1_, f32[8,256]{1,0:T(8,128)} %broadcast_in_dim.21.refs_2_.refs_1_, ...), custom_call_target="tpu_custom_call" | custom-call | tf_op jit(solution)/shard_map/pallas_call | solution.py:401
  57.2 1.6 pad_maximum_fusion.refs_1_
  58.7 34.1 %shard_map.241 = (bf16[1024,1024]{1,0:T(8,128)(2,1)}, bf16[2,1024,288]{2,1,0:T(8,128)(2,1)}) custom-call(bf16[256,1024]{1,0:T(8,128)(2,1)} %fusion.31.refs_0_, bf16[4,2,256,288]{3,2,1,0:T(8,128)(2,1)} %pad_maximum_fusion.refs_1_), custom_call_target="tpu_custom_call" | custom-call | tf_op jit(solution)/shard_map/pallas_call | solution.py:401
  92.9 2.4 fusion.109
  101.0 2.1 convolution_convert_fusion.1.refs_0_
  103.1 25.1 %shard_map.242 = (bf16[256,1024]{1,0:T(8,128)(2,1)}, bf16[256,1024]{1,0:T(8,128)(2,1)}) custom-call(bf16[1024,1024]{1,0:T(8,128)(2,1)} %convolution_convert_fusion.1.refs_0_, bf16[256,256]{1,0:T(8,128)(2,1)} %convert_element_type.170.refs_1_), custom_call_target="tpu_custom_call" | custom-call | tf_op jit(solution)/shard_map/pallas_call | solution.py:401
  129.2 28.4 %shard_map.243 = (f32[256,256]{1,0:T(8,128)}, bf16[256,1024]{1,0:T(8,128)(2,1)}) custom-call(bf16[256,1024]{1,0:T(8,128)(2,1)} %get-tuple-element.50.refs_0_, f32[256,256]{1,0:T(8,128)} %refs_1_.2), custom_call_target="tpu_custom_call" | custom-call | tf_op jit(solution)/shard_map/pallas_call | solution.py:401
  158.9 2.0 fusion.36.refs_0_
  160.9 18.5 %shard_map.244 = (bf16[1024,1024]{1,0:T(8,128)(2,1)}, bf16[288,1024]{1,0:T(8,128)(2,1)}) custom-call(bf16[256,1024]{1,0:T(8,128)(2,1)} %fusion.36.refs_0_, bf16[1152,256]{1,0:T(8,128)(2,1)} %refs_1_.3), custom_call_target="tpu_custom_call" | custom-call | tf_op jit(solution)/shard_map/pallas_call | solution.py:401
  179.5 3.8 fusion.39
  183.2 1.9 fusion.43
  185.1 4.5 multiply_convert_fusion
  189.6 1.6 convolution_convert_fusion.3
  191.2 3.3 fusion.41
  194.5 1.7 convolution_convert_fusion.2
  196.1 2.2 copy.54.refs_2_
  198.4 2.2 copy.55.refs_2_
  200.6 4.1 convolution_convert_fusion
  204.8 5.0 %add_convert_fusion.refs_0_ = bf16[1024,1024]{1,0:T(8,128)(2,1)} fusion(f32[1024,1024]{1,0:T(8,128)} %fusion.41, bf16[1024,288]{0,1:T(8,128)(2,1)S(1)} %copy-done.24, bf16[2,1024,288]{2,1,0:T(8,128)(2,1)S(1)} %copy-done.5), kind=kOutput, calls=%fused_computation.13 | convolution fusion | flops 606076928 | bytes 7667712 | tf_op jit(solution)/shard_map/dot_general | solution.py:420
  209.7 1.6 convolution_convert_fusion.4.refs_1_
  211.3 28.7 %shard_map.245 = (bf16[256,1024]{1,0:T(8,128)(2,1)}, bf16[1152,256]{1,0:T(8,128)(2,1)}, bf16[2,1024,288]{2,1,0:T(8,128)(2,1)}) custom-call(bf16[1024,1024]{1,0:T(8,128)(2,1)} %add_convert_fusion.refs_0_, bf16[288,1024]{1,0:T(8,128)(2,1)} %convolution_convert_fusion.4.refs_1_, bf16[1024,288]{1,0:T(8,128)(2,1)} %copy.54.refs_2_), custom_call_target="tpu_custom_call" | custom-call | tf_op jit(solution)/shard_map/pallas_call | solution.py:401
  240.0 2.8 reduce_sum.252.refs_1_
  242.9 35.9 %shard_map.246 = (f32[256,256]{1,0:T(8,128)}, bf16[256,1024]{1,0:T(8,128)(2,1)}, bf16[2,1024,288]{2,1,0:T(8,128)(2,1)}, bf16[2,1152,256]{2,1,0:T(8,128)(2,1)}) custom-call(bf16[256,1024]{1,0:T(8,128)(2,1)} %get-tuple-element.58.refs_0_, f32[8,256]{1,0:T(8,128)} %broadcast_in_dim.21.refs_2_.refs_1_, bf16[1024,288]{1,0:T(8,128)(2,1)} %copy.55.refs_2_, ...), custom_call_target="tpu_custom_call" | custom-call | tf_op jit(solution)/shard_map/pallas_call | solution.py:401
  278.8 2.9 reduce_sum.256.refs_1_
  283.1 20.6 %shard_map.247 = (bf16[1024,1024]{1,0:T(8,128)(2,1)}, bf16[4,256,288]{2,1,0:T(8,128)(2,1)}) custom-call(bf16[256,1024]{1,0:T(8,128)(2,1)} %fusion.28.refs_0_, bf16[1024,288]{1,0:T(8,128)(2,1)} %reduce_sum.252.refs_1_), custom_call_target="tpu_custom_call" | custom-call | tf_op jit(solution)/shard_map/pallas_call | solution.py:401
  303.8 2.4 convolution_convert_fusion.7
  306.3 1.5 copy.60
  307.8 2.7 copy.65
  310.4 3.8 fusion
  314.3 2.4 fusion.7
  319.5 2.0 fusion.20
  321.5 2.1 multiply_reduce_fusion
  323.7 1.3 convolution_convert_fusion.5
  325.1 2.0 copy.56.refs_3_
  329.3 24.7 %shard_map.248 = (bf16[256,1024]{1,0:T(8,128)(2,1)}, bf16[4,256,288]{2,1,0:T(8,128)(2,1)}, f32[2,8,2176]{2,1,0:T(8,128)}, bf16[2,1024,192]{2,1,0:T(8,128)(2,1)}, bf16[2,64,1024]{2,1,0:T(8,128)(2,1)}) custom-call(bf16[1024,1024]{1,0:T(8,128)(2,1)} %get-tuple-element.127.refs_0_, bf16[1024,288]{1,0:T(8,128)(2,1)} %reduce_sum.256.refs_1_, ...), custom_call_target="tpu_custom_call" | custom-call | tf_op jit(solution)/shard_map/pallas_call | solution.py:401
  354.0 2.4 reduce_sum.262.refs_2_
  356.4 1.7 reduce_sum.263.refs_3_
  358.1 1.6 reduce_sum.264.refs_4_
  360.5 37.9 %shard_map.249 = (bf16[4,256,256]{2,1,0:T(8,128)(2,1)}, f32[4,8,256]{2,1,0:T(8,128)}, bf16[4,256,192]{2,1,0:T(8,128)(2,1)}, bf16[256,256]{1,0:T(8,128)(2,1)}, f32[4,8,2176]{2,1,0:T(8,128)}) custom-call(bf16[256,1024]{1,0:T(8,128)(2,1)} %get-tuple-element.65.refs_0_, f32[8,256]{1,0:T(8,128)} %broadcast_in_dim.28.refs_1_, ...), custom_call_target="tpu_custom_call" | custom-call | tf_op jit(solution)/shard_map/pallas_call | solution.py:401
  399.2 1.6 reduce_sum.267.refs_0_
  400.8 6.7 %shard_map.250 = f32[4,8,2176]{2,1,0:T(8,128)} custom-call(f32[8,2176]{1,0:T(8,128)} %reduce_sum.267.refs_0_), custom_call_target="tpu_custom_call" | custom-call | tf_op jit(solution)/shard_map/pallas_call | solution.py:401
  408.5 1.7 convert_element_type.196
  414.1 1.2 convert_bitcast_fusion
  415.8 1.4 copy.66
  420.9 19.2 %reduce-scatter.5.cloned.1.call-done = bf16[256,256]{1,0:T(8,128)(2,1)} async-done(((bf16[256,1024]{1,0:T(8,128)(2,1)}), bf16[256,256]{1,0:T(8,128)(2,1)}) %reduce-scatter.5.cloned.1.call-update) | async-done | bytes 131088 | tf_op jit(solution)/shard_map/reduce_scatter | solution.py:577
  440.1 1.8 multiply_subtract_fusion
  (225 shorter events, 36.4 us)
Async XLA Ops:
  7.2 10.3 %copy-start.63 = (f32[256]{0:T(256)S(1)}, f32[256]{0:T(256)}, u32[]{:S(2)}) copy-start(f32[256]{0:T(256)} %param.23) | copy-start | bytes 3076
  7.2 10.8 %copy-start.61 = (f32[256]{0:T(256)S(1)}, f32[256]{0:T(256)}, u32[]{:S(2)}) copy-start(f32[256]{0:T(256)} %param.16) | copy-start | bytes 3076
  7.2 177.9 %all-gather.2.cloned.1.call-start = ((), (), s32[]{:S(2)}) async-start(), calls=%async_computation.4 | async-start | bytes 2621440 | tf_op jit(solution)/shard_map/all_gather | solution.py:562
  7.3 89.4 %copy-start.67 = (f32[32]{0:T(128)}, f32[32]{0:T(128)S(1)}, u32[]{:S(2)}) copy-start(f32[32]{0:T(128)S(1)} %multiply_power_fusion) | copy-start | bytes 388
  10.0 86.7 %copy-start.40 = (f32[1024]{0:T(1024)}, f32[1024]{0:T(1024)S(1)}, u32[]{:S(2)}) copy-start(f32[1024]{0:T(1024)S(1)} %fusion.94) | copy-start | bytes 12292
  14.2 41.0 %copy-start.20 = (bf16[256,1152]{1,0:T(8,128)(2,1)S(1)}, bf16[256,1152]{1,0:T(8,128)(2,1)}, u32[]{:S(2)}) copy-start(bf16[256,1152]{1,0:T(8,128)(2,1)} %param.24) | copy-start | bytes 1769476
  16.5 39.0 %copy-start.21 = (bf16[256,1152]{1,0:T(8,128)(2,1)S(1)}, bf16[256,1152]{1,0:T(8,128)(2,1)}, u32[]{:S(2)}) copy-start(bf16[256,1152]{1,0:T(8,128)(2,1)} %param.25) | copy-start | bytes 1769476
  57.2 35.7 %copy-start.29 = (bf16[1024,192]{1,0:T(8,128)(2,1)S(1)}, bf16[1024,192]{1,0:T(8,128)(2,1)}, u32[]{:S(2)}) copy-start(bf16[1024,192]{1,0:T(8,128)(2,1)} %get-tuple-element.48) | copy-start | bytes 1179652
  92.8 3.8 copy-start.57
  92.8 3.7 copy-start.59
  92.8 4.5 %copy-start.39 = (s32[1,1024]{1,0:T(1,128)S(1)}, s32[1,1024]{1,0:T(1,128)}, u32[]{:S(2)}) copy-start(s32[1,1024]{1,0:T(1,128)} %param.15) | copy-start | bytes 12292
  128.2 289.1 %reduce-scatter.3.cloned.1.call-start = ((), (), s32[]{:S(2)}) async-start(), calls=%async_computation.2 | async-start | bytes 2621440 | tf_op jit(solution)/shard_map/reduce_scatter | solution.py:578
  179.4 3.8 copy-start.2
  179.5 3.8 copy-start.3
  189.5 4.9 %copy-start.23 = (bf16[1024,288]{0,1:T(8,128)(2,1)}, bf16[1024,288]{0,1:T(8,128)(2,1)S(1)}, u32[]{:S(2)}) copy-start(bf16[1024,288]{0,1:T(8,128)(2,1)S(1)} %get-tuple-element.128) | copy-start | bytes 1769476
  200.6 4.2 copy-start.5
  200.6 4.2 copy-start.24
  204.7 235.3 %reduce-scatter.5.cloned.1.call-start = ((), (), s32[]{:S(2)}) async-start(), calls=%async_computation.3 | async-start | bytes 655360 | tf_op jit(solution)/shard_map/reduce_scatter | solution.py:577
  204.8 5.0 %copy-start.69 = (bf16[1024,1024]{1,0:T(8,128)(2,1)S(1)}, bf16[1024,1024]{1,0:T(8,128)(2,1)}, u32[]{:S(2)}) copy-start(bf16[1024,1024]{1,0:T(8,128)(2,1)} %all-gather.2.cloned.1.call-done) | copy-start | bytes 6291460
  204.8 5.0 %copy-start.70 = (bf16[1024,288]{0,1:T(8,128)(2,1)S(1)}, bf16[1024,288]{0,1:T(8,128)(2,1)}, u32[]{:S(2)}) copy-start(bf16[1024,288]{0,1:T(8,128)(2,1)} %get-tuple-element.130) | copy-start | bytes 1769476
  242.9 38.9 %copy-start = (bf16[256,1024]{1,0:T(8,128)(2,1)S(1)}, bf16[256,1024]{1,0:T(8,128)(2,1)}, u32[]{:S(2)}) copy-start(bf16[256,1024]{1,0:T(8,128)(2,1)} %get-tuple-element.52) | copy-start | bytes 1572868
  278.8 3.0 copy-start.10
  278.8 3.2 copy-start.56
  278.8 3.2 copy-start.11
  278.8 3.2 copy-start.43
  281.8 22.0 %copy-start.28 = (bf16[64,1024]{1,0:T(8,128)(2,1)S(1)}, bf16[64,1024]{1,0:T(8,128)(2,1)}, u32[]{:S(2)}) copy-start(bf16[64,1024]{1,0:T(8,128)(2,1)} %get-tuple-element.49) | copy-start | bytes 393220
  282.0 21.7 %copy-start.49 = (f32[256]{0:T(256)}, f32[256]{0:T(256)S(1)}, u32[]{:S(2)}) copy-start(f32[256]{0:T(256)S(1)} %fusion.95) | copy-start | bytes 3076
  306.3 4.1 copy-start.46
  310.4 3.8 copy-start.8
  323.7 3.4 copy-start.17
  323.7 3.4 copy-start.18
  323.7 3.4 copy-start.44
  323.7 3.8 copy-start.65
  323.7 3.8 copy-start.66
  323.7 3.8 copy-start.1
  323.7 3.8 copy-start.26
  354.0 5.7 %copy-start.12 = (bf16[256,1024]{1,0:T(8,128)(2,1)S(1)}, bf16[256,1024]{1,0:T(8,128)(2,1)}, u32[]{:S(2)}) copy-start(bf16[256,1024]{1,0:T(8,128)(2,1)} %get-tuple-element.65.refs_0_) | copy-start | bytes 1572868
  398.4 13.8 %copy-start.14 = (bf16[4,256,192]{2,1,0:T(8,128)(2,1)S(1)}, bf16[4,256,192]{2,1,0:T(8,128)(2,1)}, u32[]{:S(2)}) copy-start(bf16[4,256,192]{2,1,0:T(8,128)(2,1)} %get-tuple-element.72) | copy-start | bytes 1179652
  415.8 3.2 copy-start.15
  417.2 3.0 copy-start.54
  417.2 3.1 copy-start.38
  417.2 22.8 %copy-start.9 = (f32[256,256]{1,0:T(8,128)S(1)}, f32[256,256]{1,0:T(8,128)}, u32[]{:S(2)}) copy-start(f32[256,256]{1,0:T(8,128)} %refs_1_.2) | copy-start | bytes 786436
  417.2 22.8 %copy-start.16 = (f32[256,256]{1,0:T(8,128)S(1)}, f32[256,256]{1,0:T(8,128)}, u32[]{:S(2)}) copy-start(f32[256,256]{1,0:T(8,128)} %param.27) | copy-start | bytes 786436
  417.2 22.8 %copy-start.19 = (f32[256,256]{1,0:T(8,128)S(1)}, f32[256,256]{1,0:T(8,128)}, u32[]{:S(2)}) copy-start(f32[256,256]{1,0:T(8,128)} %get-tuple-element.60) | copy-start | bytes 786436
  417.2 22.8 %copy-start.50 = (f32[256]{0:T(256)S(1)}, f32[256]{0:T(256)}, u32[]{:S(2)}) copy-start(f32[256]{0:T(256)} %copy-done.49) | copy-start | bytes 3076
  417.2 22.8 %copy-start.52 = (f32[256]{0:T(256)S(1)}, f32[256]{0:T(256)}, u32[]{:S(2)}) copy-start(f32[256]{0:T(256)} %copy-done.51) | copy-start | bytes 3076
  417.3 22.8 %copy-start.62 = (f32[256]{0:T(256)S(1)}, f32[256]{0:T(256)}, u32[]{:S(2)}) copy-start(f32[256]{0:T(256)} %param.16) | copy-start | bytes 3076
  417.3 22.8 %copy-start.64 = (f32[256]{0:T(256)S(1)}, f32[256]{0:T(256)}, u32[]{:S(2)}) copy-start(f32[256]{0:T(256)} %param.23) | copy-start | bytes 3076
  (27 other events, 45.7 us)
Sparse Core Ops, SparseCore 0:
  128.3 22.5 all-gather.1
  204.8 38.4 reduce-scatter.2
  417.5 22.5 reduce-scatter.4

commit v3 on v2

--- a/solution.py
+++ b/solution.py
@@ -109,6 +109,17 @@
     yield
     for copy in copies:
         copy.wait()
+
+
+def pair_add_steps(plan, n, me, ins, outs, scratch):
+    sends, recvs, got = scratch
+    copy = send_to(ins[0], got, sends, recvs, 0, plan[0], lax.rem(me + 1, n))
+    yield
+    yield
+    yield
+    copy.wait()
+    flt = jnp.float32
+    outs[0][...] = (ins[0][...].astype(flt) + got[...].astype(flt)).astype(outs[0].dtype)
 
 
 def partners(me):
@@ -283,6 +294,7 @@
 
 STEPS = {
     "push": push_steps,
+    "pair_add": pair_add_steps,
     "relay_gather": relay_gather_steps,
     "relay_reduce": relay_reduce_steps,
     "reduce_gather": reduce_gather_steps,
@@ -339,7 +351,7 @@
     )
 
 
-def gather_rows(axis, array, pieces=2):
+def gather_rows(axis, array, pieces=4):
     if lax.axis_size(axis) != 4:
         return push(axis, array, None, 0)
     sems = pltpu.SemaphoreType.DMA((2 * pieces + 1,))
@@ -352,7 +364,7 @@
     )
 
 
-def reduce_rows(axis, array, pieces=2):
+def reduce_rows(axis, array, pieces=4):
     if lax.axis_size(axis) != 4:
         return push(axis, array, 0, "lead")
     rows, width = array.shape[0] // 4, array.shape[1]
@@ -444,16 +456,23 @@
     return lax.rsqrt(jnp.mean(wide * wide, axis=1, keepdims=True) + epsilon)
 
 
-def unfold(got):
-    return jnp.moveaxis(got, 0, 1).reshape(got.shape[1], -1)
-
-
 def dp_jobs(array):
-    return [push("dp", array, None, "lead")] if lax.axis_size("dp") == 2 else []
+    if lax.axis_size("dp") != 2:
+        return []
+    sems = pltpu.SemaphoreType.DMA((1,))
+    return [
+        (
+            "pair_add",
+            ("dp",),
+            [array],
+            [jax.ShapeDtypeStruct(array.shape, array.dtype)],
+            [sems, sems, pltpu.VMEM(array.shape, array.dtype)],
+        )
+    ]
 
 
 def dp_total(array, got):
-    return added(got[0]) if got else lax.psum(array, "dp").astype(jnp.float32)
+    return got[0] if got else lax.psum(array, "dp")
 
 
 def local(
@@ -485,8 +504,6 @@
     share = rows * kv_mine // kv_local
     groups = q_mine // kv_mine
     q_width, k_width = q_mine * HEAD_DIM, kv_mine * HEAD_DIM
-    ff_local = w_gate.shape[1]
-    ff_mine = ff_local // rows
     scale_factor = HEAD_DIM ** (-0.5)
     seq_local, length = segments.shape
     stream = seq_local * length
@@ -498,22 +515,17 @@
     cos_table, sin_table = rotary_tables(positions_of(documents))
 
     cot_low = cotangent.astype(low)
+    query_turned, key_turned, value_turned = w_query.T, w_key.T, w_value.T
     w_joined_parts = jnp.stack(
         [
             jnp.concatenate(
                 [
-                    w_query[:, r * q_width : (r + 1) * q_width],
-                    w_key[:, (r // share) * k_width : (r // share + 1) * k_width],
-                    w_value[:, (r // share) * k_width : (r // share + 1) * k_width],
+                    query_turned[r * q_width : (r + 1) * q_width],
+                    key_turned[(r // share) * k_width : (r // share + 1) * k_width],
+                    value_turned[(r // share) * k_width : (r // share + 1) * k_width],
                 ],
-                axis=1,
+                axis=0,
             )
-            for r in range(rows)
-        ]
-    )
-    w_pair_parts = jnp.stack(
-        [
-            jnp.stack([w[:, r * ff_mine : (r + 1) * ff_mine] for w in (w_gate, w_up)])
             for r in range(rows)
         ]
     )
@@ -522,17 +534,18 @@
         push("row", hidden_in.astype(low), None, 1),
         push("row", eight(norm_in), None, 1),
         push("row", eight(norm_mid), None, 1),
-        push("row", w_joined_parts, "lead", 0),
+        push("row", w_joined_parts, "lead", 1),
         push("row", w_out, 0, 1),
     )
     hidden_wide = hidden_row.astype(flt)
     rate_in = row_rates(hidden_wide)
-    normed_in, w_pair = exchange(
+    normed_in, w_gate_mine, w_up_mine = exchange(
         1,
         gather_rows("col", (hidden_wide * rate_in * norm_in_all[:1]).astype(low)),
-        push("row", w_pair_parts, "lead", 1),
-    )
-    projected = dot(normed_in, w_joined)
+        push("row", w_gate.T, 0, 1),
+        push("row", w_up.T, 0, 1),
+    )
+    projected = dot_turned(normed_in, w_joined)
     raw_query = projected[:, :q_width].reshape(stream, q_mine, HEAD_DIM)
     raw_key = projected[:, q_width : q_width + k_width].reshape(stream, kv_mine, HEAD_DIM)
     value_heads = projected[:, q_width + k_width :].astype(low).reshape(stream, kv_mine, HEAD_DIM)
@@ -568,56 +581,52 @@
         gather_rows("col", (resid_wide * rate_mid * norm_mid_all[:1]).astype(low)),
         push("row", w_down, 0, 1),
     )
-    gate_pre = dot(normed_mid, w_pair[0])
-    up_pre = dot(normed_mid, w_pair[1])
+    gate_pre = dot_turned(normed_mid, w_gate_mine)
+    up_pre = dot_turned(normed_mid, w_up_mine)
     sigmoid_gate = jax.nn.sigmoid(gate_pre)
     activated = gate_pre * sigmoid_gate
     swiglu = (activated * up_pre).astype(low)
     down_part = dot(swiglu, w_down_mine).astype(low)
-    down_own = lax.psum_scatter(
-        lax.psum_scatter(down_part, "col", scatter_dimension=0, tiled=True),
-        "row",
-        scatter_dimension=1,
-        tiled=True,
-    )
-    output = resid + down_own.astype(flt)
     grad_swiglu = dot_turned(cot_all, w_down_mine)
     grad_down = outer_sum(swiglu, cot_all).astype(low)
     grad_gate_act = (
         grad_swiglu * up_pre * sigmoid_gate * (1.0 + gate_pre * (1.0 - sigmoid_gate))
     ).astype(low)
     grad_up_act = (grad_swiglu * activated).astype(low)
-    mid_part = dot_turned(grad_gate_act, w_pair[0]) + dot_turned(grad_up_act, w_pair[1])
-    grad_gate = outer_sum(normed_mid, grad_gate_act).astype(low)
-    grad_up = outer_sum(normed_mid, grad_up_act).astype(low)
+    mid_part = dot(grad_gate_act, w_gate_mine) + dot(grad_up_act, w_up_mine)
+    grad_gate = outer_sum(grad_gate_act, normed_mid).astype(low)
+    grad_up = outer_sum(grad_up_act, normed_mid).astype(low)
     mid_cols, grad_down, *pair = exchange(
         5,
         reduce_rows("col", mid_part.astype(low)),
         push("row", grad_down, 1, 0),
         *dp_jobs(grad_gate),
     )
-    grad_gate = dp_total(grad_gate, pair).astype(low)
-    grad_normed_mid, scaled_row, *pair = exchange(
+    grad_gate = dp_total(grad_gate, pair)
+    grad_normed_mid, scaled_row, down_cols, *pair = exchange(
         6,
         reduce_then_gather("row", joined(mid_cols), gain=eight(norm_mid)),
+        reduce_rows("col", down_part),
         *dp_jobs(grad_up),
         *dp_jobs(grad_down),
     )
-    grad_up = dp_total(grad_up, pair[:1]).astype(low)
-    grad_down = dp_total(grad_down, pair[1:])
+    grad_up = dp_total(grad_up, pair[:1])
+    grad_down = dp_total(grad_down, pair[1:]).astype(flt)
     scaled_wide = scaled_row.astype(flt)
     mid_scale = rate_mid**3 * jnp.mean(scaled_wide * resid_wide, axis=1, keepdims=True)
     grad_resid = cotangent + rate_mid * (norm_mid * grad_normed_mid) - resid * mid_scale
     gain_mid = jnp.sum(grad_normed_mid * resid * rate_mid, axis=0)
-    resid_low, grad_gate_got = exchange(
+    resid_low, grad_gate, down_blocks = exchange(
         7,
         gather_rows(
             "col",
             (cot_row.astype(flt) + rate_mid * scaled_wide - resid_wide * mid_scale).astype(low),
         ),
-        push("row", grad_gate, 0, "lead"),
-    )
-    grad_gate = unfold(grad_gate_got).astype(flt)
+        push("row", grad_gate, 1, 0),
+        push("row", joined(down_cols), 1, "lead"),
+    )
+    grad_gate = grad_gate.T.astype(flt)
+    output = resid + added(down_blocks)
     grad_out = outer_sum(mixed, resid_low).astype(low)
     grad_mixed_heads = (
         dot_turned(resid_low, w_out_mine).astype(low).reshape(stream, kv_mine, groups, HEAD_DIM)
@@ -650,30 +659,30 @@
         ],
         axis=1,
     ).astype(low)
-    grad_joined = outer_sum(normed_in, grad_proj).astype(low)
-    in_part = dot_turned(grad_proj, w_joined)
+    grad_joined = outer_sum(grad_proj, normed_in).astype(low)
+    in_part = dot(grad_proj, w_joined)
     block_start = lax.axis_index("row") * feature_slab
     gain_in = jnp.sum(in_part * normed_in.astype(flt), axis=0) / norm_in_all[0]
     spread_mid = lax.dynamic_update_slice(jnp.zeros((model_width,), flt), gain_mid, (block_start,))
     gains = jnp.concatenate([gain_in, spread_mid, gain_query, gain_key])
-    in_cols, grad_up_got, gains_got, *pair = exchange(
+    in_cols, grad_up, gains_got, *pair = exchange(
         8,
         reduce_rows("col", in_part.astype(low)),
-        push("row", grad_up, 0, "lead"),
+        push("row", grad_up, 1, 0),
         push("dp", eight(gains), None, "lead"),
         *dp_jobs(grad_joined),
         *dp_jobs(grad_out),
     )
     in_cols = joined(in_cols)
     inner_part = jnp.sum(in_cols.astype(flt) * hidden_wide * norm_in_all[:1], axis=1)
-    grad_up = unfold(grad_up_got).astype(flt)
-    grad_joined = dp_total(grad_joined, pair[:1]).astype(low)
-    grad_out = dp_total(grad_out, pair[1:]).astype(low)
+    grad_up = grad_up.T.astype(flt)
+    grad_joined = dp_total(grad_joined, pair[:1])
+    grad_out = dp_total(grad_out, pair[1:])
     in_blocks, in_inner, joined_got, out_got, gains_got = exchange(
         9,
         push("row", in_cols, 1, "lead"),
         push("row", eight(inner_part), None, "lead"),
-        push("row", grad_joined, 0, "lead"),
+        push("row", grad_joined, 1, "lead"),
         push("row", grad_out, 1, 0),
         push("row", jnp.sum(gains_got, axis=0), None, "lead"),
     )
@@ -684,12 +693,12 @@
     grad_hidden = grad_resid + rate_in * (norm_in * grad_normed_in) - hidden_in * in_scale
 
     def shared(got):
-        summed = got.astype(flt).reshape(rows // share, share, feature_slab, k_width).sum(axis=1)
-        return unfold(summed)
-
-    grad_query = unfold(joined_got[:, :, :q_width]).astype(flt)
-    grad_key = shared(joined_got[:, :, q_width : q_width + k_width])
-    grad_value = shared(joined_got[:, :, q_width + k_width :])
+        summed = got.astype(flt).reshape(rows // share, share, k_width, feature_slab).sum(axis=1)
+        return summed.reshape(k_cols, feature_slab).T
+
+    grad_query = joined_got[:, :q_width].reshape(q_cols, feature_slab).T.astype(flt)
+    grad_key = shared(joined_got[:, q_width : q_width + k_width])
+    grad_value = shared(joined_got[:, q_width + k_width :])
     grad_out = out_got.astype(flt)
     gain_in = lax.dynamic_slice(gains, (block_start,), (feature_slab,))
     gain_mid = lax.dynamic_slice(gains, (model_width + block_start,), (feature_slab,))

time: 450 us -> 380 us (0.84)
  Pallas kernels: 295 us -> 275 us
  waiting for transfers between devices: 19.2 us -> 0.02 us
  other arithmetic: 43.5 us -> 30.4 us
  local copies, waits for them, and re-layouts: 27.1 us -> 18.6 us
  matrix products: 47.7 us -> 39.5 us
    pallas_call x11, Pallas kernels: 295 us -> 275 us  [exchange(): pl.pallas_call(functools.partial(exchange_kernel, tuple(((job[0], job[1],...]
    reduce_scatter x2 -> x0, waiting for transfers between devices: 19.2 us -> none  [the longest x1 19.2 us: local(): lax.psum_scatter(lax.psum_scatter(down_part, 'col', scatter_dimension=0,...]
    reduce_sum x6 -> x2, other arithmetic: 12.2 us -> 0.14 us  [added(): return jnp.sum(stacked.astype(jnp.float32), axis=0)]
    convert_element_type x6 -> x1, local copies, waits for them, and re-layouts: 8.51 us -> 0.84 us  [local(): joined_got[:, :q_width].reshape(q_cols, feature_slab).T.astype(flt)]
    dot_general x5, matrix products: 17.3 us -> 10.6 us  [dot_turned(): lax.dot_general(left_side, right_side, (((1,), (1,)), ((), ())), preferre...]
    unnamed x147 -> x115, local copies, waits for them, and re-layouts: 8.48 us -> 10.7 us
  transfers between devices with their start and end apart: 3 -> 1, of which waited for: 1 -> 0; matrix products, arithmetic and copies ran while one was open for 16% -> 2% of each run, Pallas kernels for 45% -> 12%
where the time goes in v3:
time: 380 us; the launch traced here: 379 us
  Pallas kernels  275 us (72%)
  matrix products  39.5 us (10%)
  other arithmetic  30.4 us (8%)
  local copies, waits for them, and re-layouts  18.6 us (5%)
  between operations  15.6 us (4%)
    pallas_call x11, Pallas kernels, exchange(): pl.pallas_call(functools.partial(exchange_kernel, tuple(((job[0], job[1],...  275 us
    dot_general x5, matrix products, dot(): return jnp.dot(left_side, right_side, preferred_element_type=jnp.float32)  10.8 us
    unnamed x115, local copies, waits for them, and re-layouts  10.7 us
    dot_general x5, matrix products, dot_turned(): lax.dot_general(left_side, right_side, (((1,), (1,)), ((), ())), preferre...  10.6 us
    dot_general x5, matrix products, outer_sum(): lax.dot_general(left_side, right_side, (((0,), (0,)), ((), ())), preferre...  9.05 us
  transfers between devices with their start and end apart: 1, of which 0 were waited for; matrix products, arithmetic and copies ran while one was open for 2% of the time, Pallas kernels for 12%

profile of v3, /device:TPU:0, one launch (start us, length us, event | category | flops | bytes accessed | tf_op | source)
XLA Modules:
  0.0 378.8 jit_solution(13890144842766414572)
XLA Ops:
  7.3 1.1 copy.35
  10.3 1.7 convert_element_type.146.refs_0_
  14.0 31.7 %shard_map.240 = (bf16[256,1024]{1,0:T(8,128)(2,1)}, f32[8,1024]{1,0:T(8,128)}, f32[8,1024]{1,0:T(8,128)}, bf16[192,1024]{1,0:T(8,128)(2,1)}, bf16[64,1024]{1,0:T(8,128)(2,1)}) custom-call(bf16[256,256]{1,0:T(8,128)(2,1)} %convert_element_type.146.refs_0_, f32[8,256]{1,0:T(8,128)} %broadcast_in_dim.20.refs_1_, f32[8,256]{1,0:T(8,128)} %broadcast_in_dim.21.refs_2_.refs_1_, ...), custom_call_target="tpu_custom_call" | custom-call | tf_op jit(solution)/shard_map/pallas_call | solution.py:413
  45.7 1.3 fusion.29
  47.8 1.1 copy.38
  48.9 1.1 copy.39
  50.0 1.0 fusion.31.refs_0_
  50.9 30.8 %shard_map.241 = (bf16[1024,1024]{1,0:T(8,128)(2,1)}, bf16[288,1024]{1,0:T(8,128)(2,1)}, bf16[288,1024]{1,0:T(8,128)(2,1)}) custom-call(bf16[256,1024]{1,0:T(8,128)(2,1)} %fusion.31.refs_0_, bf16[1152,256]{1,0:T(8,128)(2,1)} %bitcast.194, bf16[1152,256]{1,0:T(8,128)(2,1)} %bitcast.195), custom_call_target="tpu_custom_call" | custom-call | tf_op jit(solution)/shard_map/pallas_call | solution.py:413
  81.8 2.4 fusion.98
  88.2 1.0 fusion.4
  91.2 2.1 convolution_convert_fusion.1.refs_0_
  93.3 20.1 %shard_map.242 = (bf16[256,1024]{1,0:T(8,128)(2,1)}, bf16[256,1024]{1,0:T(8,128)(2,1)}) custom-call(bf16[1024,1024]{1,0:T(8,128)(2,1)} %convolution_convert_fusion.1.refs_0_, bf16[256,256]{1,0:T(8,128)(2,1)} %convert_element_type.156.refs_1_), custom_call_target="tpu_custom_call" | custom-call | tf_op jit(solution)/shard_map/pallas_call | solution.py:413
  113.4 28.1 %shard_map.243 = (f32[256,256]{1,0:T(8,128)}, bf16[256,1024]{1,0:T(8,128)(2,1)}) custom-call(bf16[256,1024]{1,0:T(8,128)(2,1)} %get-tuple-element.53.refs_0_, f32[256,256]{1,0:T(8,128)} %refs_1_.2), custom_call_target="tpu_custom_call" | custom-call | tf_op jit(solution)/shard_map/pallas_call | solution.py:413
  142.3 1.2 fusion.34
  143.6 2.0 fusion.36.refs_0_
  145.6 18.3 %shard_map.244 = (bf16[1024,1024]{1,0:T(8,128)(2,1)}, bf16[288,1024]{1,0:T(8,128)(2,1)}) custom-call(bf16[256,1024]{1,0:T(8,128)(2,1)} %fusion.36.refs_0_, bf16[1152,256]{1,0:T(8,128)(2,1)} %refs_1_.3), custom_call_target="tpu_custom_call" | custom-call | tf_op jit(solution)/shard_map/pallas_call | solution.py:413
  163.9 3.4 fusion.100
  167.4 2.7 fusion.99
  170.2 1.3 multiply_convert_fusion
  171.5 1.6 convolution_convert_fusion.3.refs_2_
  173.1 1.3 fusion.101
  174.4 1.6 convolution_convert_fusion.2.refs_3_
  176.0 2.7 convolution_convert_fusion.refs_2_
  178.7 2.7 add_convert_fusion.refs_0_
  181.4 1.6 convolution_convert_fusion.4.refs_1_
  183.0 20.6 %shard_map.245 = (bf16[256,1024]{1,0:T(8,128)(2,1)}, bf16[1152,256]{1,0:T(8,128)(2,1)}, bf16[288,1024]{1,0:T(8,128)(2,1)}) custom-call(bf16[1024,1024]{1,0:T(8,128)(2,1)} %add_convert_fusion.refs_0_, bf16[288,1024]{1,0:T(8,128)(2,1)} %convolution_convert_fusion.4.refs_1_, bf16[288,1024]{1,0:T(8,128)(2,1)} %convolution_convert_fusion.3.refs_2_), custom_call_target="tpu_custom_call" | custom-call | tf_op jit(solution)/shard_map/pallas_call | solution.py:413
  203.6 32.8 %shard_map.246 = (f32[256,256]{1,0:T(8,128)}, bf16[256,1024]{1,0:T(8,128)(2,1)}, bf16[256,1024]{1,0:T(8,128)(2,1)}, bf16[288,1024]{1,0:T(8,128)(2,1)}, bf16[1152,256]{1,0:T(8,128)(2,1)}) custom-call(bf16[256,1024]{1,0:T(8,128)(2,1)} %get-tuple-element.62.refs_0_, f32[8,256]{1,0:T(8,128)} %broadcast_in_dim.21.refs_2_.refs_1_, ...), custom_call_target="tpu_custom_call" | custom-call | tf_op jit(solution)/shard_map/pallas_call | solution.py:413
  236.5 1.3 fusion.37
  238.4 2.2 fusion.28.refs_0_
  240.6 28.6 %shard_map.247 = (bf16[1024,1024]{1,0:T(8,128)(2,1)}, bf16[1152,256]{1,0:T(8,128)(2,1)}, bf16[4,256,256]{2,1,0:T(8,128)(2,1)}) custom-call(bf16[256,1024]{1,0:T(8,128)(2,1)} %fusion.28.refs_0_, bf16[288,1024]{1,0:T(8,128)(2,1)} %get-tuple-element.65.refs_1_, bf16[256,1024]{1,0:T(8,128)(2,1)} %get-tuple-element.66.refs_2_), custom_call_target="tpu_custom_call" | custom-call | tf_op jit(solution)/shard_map/pallas_call | solution.py:413
  269.3 2.9 convolution_convert_fusion.6.refs_4_
  272.9 4.0 %fusion = (f32[1024]{0:T(1024)S(1)}, f32[1024,1024]{1,0:T(8,128)S(1)}) fusion(f32[1024]{0:T(1024)S(1)} %copy-done.29, f32[1024,1024]{1,0:T(8,128)} %copy-done.4, s32[1024]{0:T(1024)S(1)} %bitcast.207, bf16[1024,64]{0,1:T(8,128)(2,1)S(1)} %convolution_convert_fusion.7, f32[1024,192]{0,1:T(8,128)S(1)} %fusion.98), kind=kOutput, calls=%fused_computation.2 | convolution fusion | flops 142605312 | bytes 8667136 | tf_op jit(solution)/shard_map/qkgd,skd->kgqs/dot_general | solution.py:637
  276.9 2.4 fusion.7
  280.6 2.0 fusion.20
  284.2 1.4 convolution_convert_fusion.5.refs_3_
  285.6 2.1 multiply_reduce_fusion
  288.8 23.1 %shard_map.248 = (bf16[256,1024]{1,0:T(8,128)(2,1)}, bf16[1152,256]{1,0:T(8,128)(2,1)}, f32[2,8,2176]{2,1,0:T(8,128)}, bf16[192,1024]{1,0:T(8,128)(2,1)}, bf16[64,1024]{1,0:T(8,128)(2,1)}) custom-call(bf16[1024,1024]{1,0:T(8,128)(2,1)} %get-tuple-element.120.refs_0_, bf16[288,1024]{1,0:T(8,128)(2,1)} %get-tuple-element.70.refs_1_, ...), custom_call_target="tpu_custom_call" | custom-call | tf_op jit(solution)/shard_map/pallas_call | solution.py:413
  312.0 1.6 reduce_sum.213.refs_4_
  313.5 1.3 fusion.33
  315.4 33.7 %shard_map.249 = (bf16[4,256,256]{2,1,0:T(8,128)(2,1)}, f32[4,8,256]{2,1,0:T(8,128)}, bf16[4,192,256]{2,1,0:T(8,128)(2,1)}, bf16[256,256]{1,0:T(8,128)(2,1)}, f32[4,8,2176]{2,1,0:T(8,128)}) custom-call(bf16[256,1024]{1,0:T(8,128)(2,1)} %get-tuple-element.71.refs_0_, f32[8,256]{1,0:T(8,128)} %broadcast_in_dim.28.refs_1_, ...), custom_call_target="tpu_custom_call" | custom-call | tf_op jit(solution)/shard_map/pallas_call | solution.py:413
  349.2 1.7 reduce_sum.216.refs_0_
  350.8 6.8 %shard_map.250 = f32[4,8,2176]{2,1,0:T(8,128)} custom-call(f32[8,2176]{1,0:T(8,128)} %reduce_sum.216.refs_0_), custom_call_target="tpu_custom_call" | custom-call | tf_op jit(solution)/shard_map/pallas_call | solution.py:413
  357.6 1.0 reduce_sum.217
  360.1 1.0 convert_reduce_fusion.2
  362.2 1.4 copy.44
  366.7 1.2 convert_bitcast_fusion.1
  368.0 1.4 copy.43
  369.4 1.1 convert_element_type.187
  (173 shorter events, 24.1 us)
Async XLA Ops:
  7.2 5.6 %copy-start.45 = (f32[256]{0:T(256)S(1)}, f32[256]{0:T(256)}, u32[]{:S(2)}) copy-start(f32[256]{0:T(256)} %param.23) | copy-start | bytes 3076
  7.2 6.2 %copy-start.43 = (f32[256]{0:T(256)S(1)}, f32[256]{0:T(256)}, u32[]{:S(2)}) copy-start(f32[256]{0:T(256)} %param.16) | copy-start | bytes 3076
  7.2 40.6 %copy-start.15 = (bf16[256,1152]{1,0:T(8,128)(2,1)S(1)}, bf16[256,1152]{1,0:T(8,128)(2,1)}, u32[]{:S(2)}) copy-start(bf16[256,1152]{1,0:T(8,128)(2,1)} %param.24) | copy-start | bytes 1769476
  7.2 160.1 %all-gather.2.cloned.1.call-start = ((), (), s32[]{:S(2)}) async-start(), calls=%async_computation | async-start | bytes 2621440 | tf_op jit(solution)/shard_map/all_gather | solution.py:575
  7.3 80.3 %copy-start.47 = (f32[32]{0:T(128)}, f32[32]{0:T(128)S(1)}, u32[]{:S(2)}) copy-start(f32[32]{0:T(128)S(1)} %multiply_power_fusion) | copy-start | bytes 388
  10.3 38.6 %copy-start.16 = (bf16[256,1152]{1,0:T(8,128)(2,1)S(1)}, bf16[256,1152]{1,0:T(8,128)(2,1)}, u32[]{:S(2)}) copy-start(bf16[256,1152]{1,0:T(8,128)(2,1)} %param.25) | copy-start | bytes 1769476
  45.7 4.2 %copy-start.3 = (bf16[256,1024]{1,0:T(8,128)(2,1)S(1)}, bf16[256,1024]{1,0:T(8,128)(2,1)}, u32[]{:S(2)}) copy-start(bf16[256,1024]{1,0:T(8,128)(2,1)} %get-tuple-element.48) | copy-start | bytes 1572868
  47.0 34.7 %copy-start.36 = (f32[256]{0:T(256)}, f32[256]{0:T(256)S(1)}, u32[]{:S(2)}) copy-start(f32[256]{0:T(256)S(1)} %fusion.29) | copy-start | bytes 3076
  47.1 34.7 %copy-start.34 = (f32[256]{0:T(256)}, f32[256]{0:T(256)S(1)}, u32[]{:S(2)}) copy-start(f32[256]{0:T(256)S(1)} %add_rsqrt_fusion.3) | copy-start | bytes 3076
  48.9 32.9 %copy-start.20 = (bf16[192,1024]{1,0:T(8,128)(2,1)S(1)}, bf16[192,1024]{1,0:T(8,128)(2,1)}, u32[]{:S(2)}) copy-start(bf16[192,1024]{1,0:T(8,128)(2,1)} %get-tuple-element.51) | copy-start | bytes 1179652
  81.8 4.3 %copy-start.23 = (s32[1,1024]{1,0:T(1,128)S(1)}, s32[1,1024]{1,0:T(1,128)}, u32[]{:S(2)}) copy-start(s32[1,1024]{1,0:T(1,128)} %param.15) | copy-start | bytes 12292
  81.8 5.7 %copy-start.39 = (f32[64]{0:T(128)S(1)}, f32[64]{0:T(128)}, u32[]{:S(2)}) copy-start(f32[64]{0:T(128)} %param.21) | copy-start | bytes 772
  81.8 5.7 %copy-start.41 = (f32[64]{0:T(128)S(1)}, f32[64]{0:T(128)}, u32[]{:S(2)}) copy-start(f32[64]{0:T(128)} %param.20) | copy-start | bytes 772
  89.2 2.0 copy-start.4
  89.2 2.0 copy-start.28
  113.4 50.5 %copy-start.12 = (bf16[288,1024]{1,0:T(8,128)(2,1)S(1)}, bf16[288,1024]{1,0:T(8,128)(2,1)}, u32[]{:S(2)}) copy-start(bf16[288,1024]{1,0:T(8,128)(2,1)} %get-tuple-element.61) | copy-start | bytes 1769476
  143.5 23.8 %copy-start.38 = (f32[256]{0:T(256)}, f32[256]{0:T(256)S(1)}, u32[]{:S(2)}) copy-start(f32[256]{0:T(256)S(1)} %fusion.34) | copy-start | bytes 3076
  143.5 23.8 %copy-start.26 = (f32[256]{0:T(256)}, f32[256]{0:T(256)S(1)}, u32[]{:S(2)}) copy-start(f32[256]{0:T(256)S(1)} %add_rsqrt_fusion.2) | copy-start | bytes 3076
  167.3 2.7 copy-start.11
  167.3 2.7 copy-start.50
  167.3 2.9 copy-start.52
  178.7 2.7 copy-start.49
  203.6 32.9 %copy-start = (bf16[256,1024]{1,0:T(8,128)(2,1)S(1)}, bf16[256,1024]{1,0:T(8,128)(2,1)}, u32[]{:S(2)}) copy-start(bf16[256,1024]{1,0:T(8,128)(2,1)} %get-tuple-element.56) | copy-start | bytes 1572868
  203.6 34.8 %copy-start.7 = (bf16[256,1024]{1,0:T(8,128)(2,1)S(1)}, bf16[256,1024]{1,0:T(8,128)(2,1)}, u32[]{:S(2)}) copy-start(bf16[256,1024]{1,0:T(8,128)(2,1)} %get-tuple-element.55) | copy-start | bytes 1572868
  238.4 2.2 copy-start.32
  269.2 2.9 copy-start.1
  269.2 3.6 copy-start.29
  272.9 4.0 %copy-start.5 = (f32[1024,1024]{1,0:T(8,128)S(1)}, f32[1024,1024]{1,0:T(8,128)}, u32[]{:S(2)}) copy-start(f32[1024,1024]{1,0:T(8,128)} %copy-done.4) | copy-start | bytes 12582916
  280.6 2.0 copy-start.25
  280.6 2.0 copy-start.48
  280.6 2.6 copy-start.40
  280.6 2.6 copy-start.42
  285.6 2.1 copy-start.9
  285.6 2.1 copy-start.10
  285.6 2.1 copy-start.27
  313.5 48.4 %copy-start.37 = (f32[256]{0:T(256)S(1)}, f32[256]{0:T(256)}, u32[]{:S(2)}) copy-start(f32[256]{0:T(256)} %copy-done.36) | copy-start | bytes 3076
  314.8 47.2 %copy-start.18 = (bf16[4,256,256]{2,1,0:T(8,128)(2,1)S(1)}, bf16[4,256,256]{2,1,0:T(8,128)(2,1)}, u32[]{:S(2)}) copy-start(bf16[4,256,256]{2,1,0:T(8,128)(2,1)} %get-tuple-element.67) | copy-start | bytes 1572868
  315.4 46.7 %copy-start.14 = (bf16[1152,256]{1,0:T(8,128)(2,1)S(1)}, bf16[1152,256]{1,0:T(8,128)(2,1)}, u32[]{:S(2)}) copy-start(bf16[1152,256]{1,0:T(8,128)(2,1)} %get-tuple-element.81) | copy-start | bytes 1769476
  349.2 12.8 %copy-start.19 = (bf16[4,256,256]{2,1,0:T(8,128)(2,1)S(1)}, bf16[4,256,256]{2,1,0:T(8,128)(2,1)}, u32[]{:S(2)}) copy-start(bf16[4,256,256]{2,1,0:T(8,128)(2,1)} %get-tuple-element.75) | copy-start | bytes 1572868
  358.6 3.6 copy-start.22
  362.2 3.8 copy-start.21
  366.7 2.7 copy-start.13
  367.9 2.5 copy-start.6
  367.9 2.5 copy-start.33
  368.0 2.5 copy-start.35
  368.0 2.5 copy-start.44
  368.0 2.5 copy-start.46
  369.4 2.0 slice-start
  (7 other events, 9.0 us)
Sparse Core Ops, SparseCore 0:
  113.5 22.2 all-gather.1
